TPU v7x, 512 devices: a whole 4x4x16 slice. The times are simulated.
512 devices in a mesh: seq: 32 (over z, core), chan: 16 (over x, y).
Axes of the slice: x: 4, y: 4, z: 16, core: 2. Of those that a mesh axis runs over, the one named last changes fastest.
Arguments:
- loaded: bfloat16 [3, 32768, 4096], P(None, 'seq', 'chan'), may hold values from -6 to 6
- dest_tiles: int32 [1024], P('seq'), may hold values from 0 to 511, as said below
- tile_counts: int32 [32], P('seq'), may hold values from 8 to 32, as said below
- segments: int32 [16384], P('seq'), may hold values from 0 to 63, never falling along the last dimension, each value on 1 to 1024 neighbouring positions
- short_filters: float32 [3, 7, 4096], P(None, None, 'chan')
- long_filters: bfloat16 [256, 16384], P('chan', 'seq')
- skip_gain: float32 [4096], P('chan'), may hold values from 0.5 to 1.5
- norm_gain: float32 [4096], P('chan'), may hold values from 0.5 to 1.5
Outputs:
- layer_out: bfloat16 [16384, 4096], P('seq', 'chan')
Inputs may be any that keep to these rules, and one draw needn't show every extreme that they name: Index s of seq holds tile_counts[s] tiles in its first slots; the busiest holds exactly 32, and every count is a multiple of 2. `dest_tiles`: entry s * 32 + j names the tile held in slot j of index s when j < tile_counts[s]; later slots name arbitrary tiles. The used slots name every tile exactly once. Tile d belongs to index d // 16 of seq, and one index holds either none or exactly 2 tiles of any one index.
All inputs are finite; a program needn't handle non-finite values.
Results may differ from a plain program's by a relative error of at most 0.0057.
Values may be sent and summed in bfloat16 or wider, within the bound.
No kernel may reach another device: no remote copies, remote signals or barrier semaphores. Data moves between devices by JAX's collectives and lax.ppermute only.
A program may use at most 64 MiB of HBM per device.

v0:
```python
import math

import jax
import jax.numpy as jnp
from jax import lax
from jax.sharding import PartitionSpec as P

CHANNELS = 4096
TILES_DEV = 16


highest = lax.Precision.HIGHEST


def from_behind(block, axis, distance):
    devices = range(lax.axis_size(axis))
    route = [(i - distance, i) for i in devices if i - distance in devices]
    return lax.ppermute(block, axis, route)


def contract(einsum_form, left_side, right_side):
    return jnp.einsum(einsum_form, left_side, right_side, precision=highest)


def angles(first, second, period):
    turn_count = first[:, None] * second[None, :] % period
    return 2.0 * math.pi / period * turn_count.astype(jnp.float32)


def complex_apply(einsum_form, table_re, table_im, value_re, value_im):
    out_re = contract(einsum_form, table_re, value_re) - contract(einsum_form, table_im, value_im)
    out_im = contract(einsum_form, table_re, value_im) + contract(einsum_form, table_im, value_re)
    return (out_re, out_im)


def arrange_tiles(loaded, dest_tiles, tile_counts, devices):
    slot_count = dest_tiles.shape[0]
    chans_here = loaded.shape[2]
    tile_rows = loaded.shape[1] // slot_count
    per_pair = 4 * TILES_DEV // devices
    slot_ids = jnp.arange(slot_count, dtype=jnp.int32)
    valid_slot = slot_ids < tile_counts[0]
    owner_device = dest_tiles // TILES_DEV
    hit_table = (
        (owner_device[:, None] == jnp.arange(devices, dtype=jnp.int32)[None, :])
        & valid_slot[:, None]
    ).astype(jnp.int32)
    before = jnp.cumsum(hit_table, axis=0) - 1
    send_slot = owner_device * per_pair + jnp.sum(before * hit_table, axis=1)
    chosen = (
        send_slot[None, :] == jnp.arange(devices * per_pair, dtype=jnp.int32)[:, None]
    ) & valid_slot[None, :]
    slot_data = loaded.reshape(3, slot_count, tile_rows * chans_here)
    packed = jnp.einsum(
        "sj,ijx->isx", chosen.astype(jnp.bfloat16), slot_data, preferred_element_type=jnp.float32
    ).astype(jnp.bfloat16)
    local_ids = (dest_tiles % TILES_DEV).astype(jnp.float32)
    labels = jnp.where(
        jnp.any(chosen, axis=1), jnp.sum(jnp.where(chosen, local_ids[None, :], 0.0), axis=1), -1.0
    ).astype(jnp.bfloat16)
    received, tile_labels = (
        lax.all_to_all(
            packed.reshape(3, devices, per_pair, tile_rows * chans_here),
            "seq",
            split_axis=1,
            concat_axis=1,
            tiled=True,
        ),
        lax.all_to_all(
            labels.reshape(1, devices, per_pair), "seq", split_axis=1, concat_axis=1, tiled=True
        ),
    )
    pick_table = (
        tile_labels.reshape(-1)[None, :].astype(jnp.float32)
        == jnp.arange(TILES_DEV, dtype=jnp.float32)[:, None]
    ).astype(jnp.bfloat16)
    placed = jnp.einsum(
        "ts,isx->itx",
        pick_table,
        received.reshape(3, devices * per_pair, tile_rows * chans_here),
        preferred_element_type=jnp.float32,
    )
    return placed.astype(jnp.bfloat16).reshape(3, TILES_DEV * tile_rows, chans_here)


def sequence_conv(mixed_rows, kernels, devices):
    seq_rows, chans_here = mixed_rows.shape
    filter_count = kernels.shape[0]
    block_rows = seq_rows // devices
    period = 2 * seq_rows * devices
    position = lax.axis_index("seq")
    signal, kernel_part = (
        lax.all_to_all(
            mixed_rows.reshape(devices, block_rows, chans_here),
            "seq",
            split_axis=0,
            concat_axis=0,
            tiled=True,
        ),
        lax.all_to_all(
            kernels.T.reshape(devices, block_rows, filter_count),
            "seq",
            split_axis=0,
            concat_axis=0,
            tiled=True,
        ),
    )
    outer_angle = angles(
        jnp.arange(2 * devices, dtype=jnp.int32), jnp.arange(devices, dtype=jnp.int32), 2 * devices
    )
    outer_cos = jnp.cos(outer_angle)
    outer_sin = jnp.sin(outer_angle)
    local_index = position * block_rows + jnp.arange(block_rows, dtype=jnp.int32)
    twist_angle = angles(jnp.arange(2 * devices, dtype=jnp.int32), local_index, period)
    twist_cos = jnp.cos(twist_angle)[:, :, None]
    twist_sin = -jnp.sin(twist_angle)[:, :, None]

    def forward_outer(value_entries):
        real_in = value_entries.astype(jnp.float32)
        first_re = contract("kp,pmc->kmc", outer_cos, real_in)
        first_im = -contract("kp,pmc->kmc", outer_sin, real_in)
        rot_re = first_re * twist_cos - first_im * twist_sin
        rot_im = first_re * twist_sin + first_im * twist_cos
        stacked = jnp.stack([rot_re, rot_im])
        return stacked.reshape(2, devices, 2, block_rows, value_entries.shape[2])

    data_cols, kern_cols = (
        lax.all_to_all(forward_outer(signal), "seq", split_axis=1, concat_axis=3, tiled=True),
        lax.all_to_all(forward_outer(kernel_part), "seq", split_axis=1, concat_axis=3, tiled=True),
    )
    data_cols = data_cols.reshape(2, 2, seq_rows, chans_here)
    kern_cols = kern_cols.reshape(2, 2, seq_rows, filter_count)
    inner_angle = angles(
        jnp.arange(seq_rows, dtype=jnp.int32), jnp.arange(seq_rows, dtype=jnp.int32), seq_rows
    )
    inner_cos = jnp.cos(inner_angle)
    inner_sin = jnp.sin(inner_angle)
    spec_re, spec_im = complex_apply(
        "km,bmc->bkc", inner_cos, -inner_sin, data_cols[0], data_cols[1]
    )
    ker_re, ker_im = complex_apply("km,bmc->bkc", inner_cos, -inner_sin, kern_cols[0], kern_cols[1])
    ker_re = jnp.repeat(ker_re, chans_here // filter_count, axis=2)
    ker_im = jnp.repeat(ker_im, chans_here // filter_count, axis=2)
    prod_re = spec_re * ker_re - spec_im * ker_im
    prod_im = spec_re * ker_im + spec_im * ker_re
    back_re, back_im = complex_apply("mk,bkc->bmc", inner_cos, inner_sin, prod_re, prod_im)
    held_freq = 2 * position + jnp.arange(2, dtype=jnp.int32)
    untwist = angles(held_freq, jnp.arange(seq_rows, dtype=jnp.int32), period)
    untwist_cos = jnp.cos(untwist)[:, :, None]
    untwist_sin = jnp.sin(untwist)[:, :, None]
    rot_re = back_re * untwist_cos - back_im * untwist_sin
    rot_im = back_re * untwist_sin + back_im * untwist_cos
    stacked = jnp.stack([rot_re, rot_im]).reshape(2, 2, devices, block_rows, chans_here)
    gathered = lax.all_to_all(stacked, "seq", split_axis=2, concat_axis=1, tiled=True)
    final_angle = angles(
        jnp.arange(devices, dtype=jnp.int32), jnp.arange(2 * devices, dtype=jnp.int32), 2 * devices
    )
    result = (
        contract("pk,kmc->pmc", jnp.cos(final_angle), gathered[0, :, 0])
        - contract("pk,kmc->pmc", jnp.sin(final_angle), gathered[1, :, 0])
    ) / period
    returned = lax.all_to_all(result, "seq", split_axis=0, concat_axis=1, tiled=True)
    return returned.reshape(seq_rows, chans_here)


def local(
    loaded, dest_tiles, tile_counts, segments, short_filters, long_filters, skip_gain, norm_gain
):
    devices = lax.axis_size("seq")
    arranged = arrange_tiles(loaded, dest_tiles, tile_counts, devices)
    seq_rows = arranged.shape[1]
    chans_here = arranged.shape[2]
    reach_rows = short_filters.shape[1] - 1
    current = segments.astype(jnp.float32)
    rim_rows, rim_segments = from_behind(
        (
            arranged[:, seq_rows - reach_rows :, :].astype(jnp.float32),
            current[seq_rows - reach_rows :],
        ),
        "seq",
        1,
    )
    extended = jnp.concatenate([rim_rows.astype(jnp.bfloat16), arranged], axis=1)
    segment_ext = jnp.concatenate([rim_segments, current])
    filtered = jnp.zeros((3, seq_rows, chans_here), jnp.float32)
    for offset in range(reach_rows + 1):
        begin_row = reach_rows - offset
        window = extended[:, begin_row : begin_row + seq_rows, :].astype(jnp.float32)
        same_doc = segment_ext[begin_row : begin_row + seq_rows] == current
        filtered = (
            filtered
            + jnp.where(same_doc[None, :, None], window, 0.0)
            * short_filters[:, offset, :][:, None, :]
        )
    gate_rows = lax.optimization_barrier(filtered[0].astype(jnp.bfloat16))
    mixed_rows = lax.optimization_barrier((filtered[1] * filtered[2]).astype(jnp.bfloat16))
    convolved = sequence_conv(mixed_rows, long_filters, devices)
    gated_rows = gate_rows.astype(jnp.float32) * (
        convolved + skip_gain[None, :] * mixed_rows.astype(jnp.float32)
    )
    row_power = lax.psum(jnp.sum(gated_rows * gated_rows, axis=1), "chan") / CHANNELS
    return (gated_rows * lax.rsqrt(row_power + 1e-06)[:, None] * norm_gain[None, :]).astype(
        jnp.bfloat16
    )


def solution(mesh):
    return jax.shard_map(
        local,
        mesh=mesh,
        in_specs=(
            P(None, "seq", "chan"),
            P("seq"),
            P("seq"),
            P("seq"),
            P(None, None, "chan"),
            P("chan", "seq"),
            P("chan"),
            P("chan"),
        ),
        out_specs=P("seq", "chan"),
        check_vma=False,
    )
```

profile of v0, /device:TPU:32, one launch (start us, length us, event | category | flops | bytes accessed | tf_op | source)
XLA Modules:
  0.0 627.8 jit_solution(3770641528342404631)
XLA Ops:
  0.7 0.7 fusion.117
  1.9 0.7 convert_element_type.186
  2.6 15.4 %all-to-all-start.1 = ((bf16[1,32,2]{2,0,1:T(2,128)(2,1)}), bf16[1,32,2]{2,0,1:T(2,128)(2,1)S(1)}, u32[]{:S(2)}, u32[]{:S(2)}) async-start(bf16[1,32,2]{2,0,1:T(2,128)(2,1)} %convert_element_type.186), calls=%async_computation.1 | async-start | bytes 32768 | tf_op jit(solution)/shard_map/all_to_all | solution.py:69
  18.0 3.8 reshape.233
  21.8 2.5 fusion
  24.3 3.8 reshape.234
  28.0 8.8 %copy.32 = bf16[3,32,2,8192]{3,2,0,1:T(2,128)(2,1)} copy(bf16[3,32,2,8192]{3,2,1,0:T(2,128)(2,1)} %reshape.234) | data formatting | bytes 6291456 | tf_op jit(solution)/shard_map/reshape | solution.py:63
  36.8 12.3 %all-to-all-start = ((bf16[3,32,2,8192]{3,2,0,1:T(2,128)(2,1)}), bf16[3,32,2,8192]{3,2,0,1:T(2,128)(2,1)S(1)}, u32[]{:S(2)}, u32[]{:S(2)}) async-start(bf16[3,32,2,8192]{3,2,0,1:T(2,128)(2,1)} %copy.32), calls=%async_computation | async-start | bytes 6291456 | tf_op jit(solution)/shard_map/all_to_all | solution.py:62
  49.3 2.0 collective-permute-start
  51.5 0.7 reshape.263
  52.3 126.8 %collective-permute-done = f32[6]{0:T(128)S(1)} collective-permute-done((f32[6]{0:T(128)S(1)}, f32[6]{0:T(128)S(1)}, u32[]{:S(2)}, u32[]{:S(2)}) %collective-permute-start) | collective-permute-done | bytes 56 | tf_op jit(solution)/shard_map/ppermute | solution.py:18
  179.3 15.1 %all-to-all-done = bf16[3,32,2,8192]{3,2,0,1:T(2,128)(2,1)S(1)} async-done(((bf16[3,32,2,8192]{3,2,0,1:T(2,128)(2,1)}), bf16[3,32,2,8192]{3,2,0,1:T(2,128)(2,1)S(1)}, u32[]{:S(2)}, u32[]{:S(2)}) %all-to-all-start) | async-done | bytes 3145760 | tf_op jit(solution)/shard_map/all_to_all | solution.py:62
  194.4 3.6 all-to-all-start.4
  197.9 4.5 copy.33
  202.5 4.0 reshape.235
  206.5 1.4 fusion.1
  207.9 1.4 reshape.236
  209.4 2.0 collective-permute-start.1
  211.5 3.0 collective-permute-done.1
  214.4 2.2 multiply_add_fusion
  216.6 1.2 copy-done
  217.8 0.8 fusion.62
  218.6 13.3 %all-to-all-start.2 = ((bf16[32,16,256]{2,1,0:T(8,128)(2,1)}), bf16[32,16,256]{2,1,0:T(8,128)(2,1)S(1)}, u32[]{:S(2)}, u32[]{:S(2)}) async-start(bf16[32,16,256]{2,1,0:T(8,128)(2,1)} %bitcast.9), calls=%async_computation.2 | async-start | bytes 524288 | tf_op jit(solution)/shard_map/all_to_all | solution.py:93
  233.6 1.0 reshape.265
  234.6 18.2 %all-to-all-done.2 = bf16[32,16,256]{2,1,0:T(8,128)(2,1)S(1)} async-done(((bf16[32,16,256]{2,1,0:T(8,128)(2,1)}), bf16[32,16,256]{2,1,0:T(8,128)(2,1)S(1)}, u32[]{:S(2)}, u32[]{:S(2)}) %all-to-all-start.2) | async-done | bytes 262176 | tf_op jit(solution)/shard_map/all_to_all | solution.py:93
  252.8 5.5 all-to-all-start.5
  258.4 0.7 fusion.64
  259.1 1.0 multiply_subtract_fusion
  260.1 0.6 copy.62
  260.7 0.6 copy.63
  261.3 1.5 pad_maximum_fusion
  262.8 11.6 %all-to-all-done.5 = f32[32,1,1024]{2,1,0:T(1,128)S(1)} async-done(((f32[32,1,1024]{2,1,0:T(1,128)}), f32[32,1,1024]{2,1,0:T(1,128)S(1)}, u32[]{:S(2)}, u32[]{:S(2)}) %all-to-all-start.5) | async-done | bytes 131104 | tf_op jit(solution)/shard_map/all_to_all | solution.py:129
  274.5 5.1 all-to-all-start.3
  279.7 0.6 broadcast.321
  280.3 0.9 reduce.4
  281.2 0.4 reshape.266
  281.7 0.9 fusion.192
  282.6 1.5 copy.48
  284.3 0.4 copy.49
  285.0 5.3 fusion.29
  290.3 5.3 fusion.25
  295.5 5.3 fusion.6
  300.9 5.3 fusion.5
  306.2 73.4 %all-to-all-done.3 = f32[2,32,2,16,256]{4,3,2,0,1:T(8,128)S(1)} async-done(((f32[2,32,2,16,256]{4,3,2,0,1:T(8,128)}), f32[2,32,2,16,256]{4,3,2,0,1:T(8,128)S(1)}, u32[]{:S(2)}, u32[]{:S(2)}) %all-to-all-start.3) | async-done | bytes 2097184 | tf_op jit(solution)/shard_map/all_to_all | solution.py:128
  380.0 7.5 %fusion.27 = f32[2,256,512]{2,1,0:T(8,128)S(1)} fusion(f32[2,512,256]{2,1,0:T(8,128)S(1)} %bitcast.175), kind=kOutput, calls=%fused_computation.54 | convolution fusion | flops 1614282752 | bytes 2097152 | tf_op jit(solution)/shard_map/km,bmc->bkc/dot_general | solution.py:22
  387.6 7.7 %fusion.31 = f32[2,256,512]{2,1,0:T(8,128)S(1)} fusion(f32[2,512,256]{2,1,0:T(8,128)S(1)} %bitcast.179), kind=kOutput, calls=%fused_computation.58 | convolution fusion | flops 1614282752 | bytes 2097152 | tf_op jit(solution)/shard_map/km,bmc->bkc/dot_general | solution.py:22
  395.3 7.6 %fusion.2 = f32[2,512,256]{1,2,0:T(8,128)S(1)} fusion(f32[2,256,512]{2,1,0:T(8,128)S(1)} %fusion.27, f32[2,512,256]{2,1,0:T(8,128)S(1)} %bitcast.180), kind=kOutput, calls=%fused_computation.23 | convolution fusion | flops 1614807040 | bytes 3145728 | tf_op jit(solution)/shard_map/km,bmc->bkc/dot_general | solution.py:22
  402.9 7.8 %fusion.10 = (f32[2,512,256]{1,2,0:T(8,128)S(1)}, f32[2,512,256]{1,2,0:T(8,128)S(1)}) fusion(f32[2,512,256]{1,2,0:T(8,128)S(1)} %fusion.2, f32[2,512,16]{1,2,0:T(8,128)S(1)} %fusion.5, f32[2,512,16]{1,2,0:T(8,128)S(1)} %fusion.6, f32[2,256,512]{2,1,0:T(8,128)S(1)} %fusion.31, f32[2,512,256]{2,1,0:T(8,128)S(1)} %bitcast.176), kind=kOutput, calls=%fused_computation.36 | convolution fusion | flops 1616379904 | bytes 5373952 | tf_op jit(solution)/shard_map/km,bmc->bkc/dot_general | solution.py:22
  410.7 6.5 %fusion.23 = f32[2,256,512]{2,1,0:T(8,128)S(1)} fusion(f32[2,512,256]{1,2,0:T(8,128)S(1)} %get-tuple-element.5), kind=kOutput, calls=%fused_computation.50 | convolution fusion | flops 1614282752 | bytes 2097152 | tf_op jit(solution)/shard_map/mk,bkc->bmc/dot_general | solution.py:22
  417.3 6.3 %fusion.21 = f32[2,256,512]{2,1,0:T(8,128)S(1)} fusion(f32[2,512,256]{1,2,0:T(8,128)S(1)} %get-tuple-element.6), kind=kOutput, calls=%fused_computation.48 | convolution fusion | flops 1614282752 | bytes 2097152 | tf_op jit(solution)/shard_map/mk,bkc->bmc/dot_general | solution.py:22
  423.6 6.3 %convolution_add_fusion = f32[2,256,512]{2,1,0:T(8,128)S(1)} fusion(f32[2,256,512]{2,1,0:T(8,128)S(1)} %fusion.21, f32[2,512,256]{1,2,0:T(8,128)S(1)} %get-tuple-element.5), kind=kOutput, calls=%fused_computation.20 | convolution fusion | flops 1614544896 | bytes 3145728 | tf_op jit(solution)/shard_map/mk,bkc->bmc/dot_general | solution.py:22
  430.0 6.7 %subtract_bitcast_fusion = (f32[2,512,256]{1,2,0:T(8,128)S(1)}, f32[2,512,256]{1,2,0:T(8,128)S(1)}) fusion(f32[2,256,512]{2,1,0:T(8,128)S(1)} %convolution_add_fusion, f32[2,512]{1,0:T(2,128)S(1)} %get-tuple-element.34, f32[2,512]{1,0:T(2,128)S(1)} %get-tuple-element.33, f32[2,256,512]{2,1,0:T(8,128)S(1)} %fusion.23, f32[2,512,256]{1,2,0:T(8,128)S(1)} %get-tuple-element.6), kind=kOutput, calls=%fused_computation.61 | convolution fusion | flops 1616117760 | bytes 5251072 | tf_op jit(solution)/shard_map/mk,bkc->bmc/dot_general | solution.py:22
  436.7 0.3 copy.52
  437.1 0.3 copy.53
  437.8 103.4 %all_to_all.74 = f32[2,2,32,16,256]{4,3,1,0,2:T(8,128)S(1)} all-to-all(f32[2,2,32,16,256]{4,3,1,0,2:T(8,128)S(1)} %copy.54), channel_id=1, replica_groups=mesh['seq'=32,'chan'=16] {'seq'}, dimensions={2} | all-to-all | bytes 4194304 | tf_op jit(solution)/shard_map/all_to_all | solution.py:154
  541.6 1.3 fusion.13
  542.8 1.3 fusion.4
  544.1 1.1 copy.57
  545.2 6.4 %all-to-all-start.7 = ((f32[32,16,256]{2,1,0:T(8,128)}), f32[32,16,256]{2,1,0:T(8,128)S(1)}, u32[]{:S(2)}, u32[]{:S(2)}) async-start(f32[32,16,256]{2,1,0:T(8,128)} %copy.57), calls=%async_computation.7 | async-start | bytes 1048576 | tf_op jit(solution)/shard_map/all_to_all | solution.py:162
  551.7 1.1 fusion.61
  552.7 31.0 %all-to-all-done.7 = f32[32,16,256]{2,1,0:T(8,128)S(1)} async-done(((f32[32,16,256]{2,1,0:T(8,128)}), f32[32,16,256]{2,1,0:T(8,128)S(1)}, u32[]{:S(2)}, u32[]{:S(2)}) %all-to-all-start.7) | async-done | bytes 524320 | tf_op jit(solution)/shard_map/all_to_all | solution.py:162
  583.8 1.1 multiply_reduce_fusion
  584.9 40.7 %psum.7 = f32[512]{0:T(512)S(1)} all-reduce(f32[512]{0:T(512)S(1)} %multiply_reduce_fusion), channel_id=1, replica_groups=mesh['seq'=32,'chan'=16] {'chan'}, use_global_device_ids=true, to_apply=%region_5.6 | all-reduce | flops 512 | bytes 4096 | tf_op jit(solution)/shard_map/psum | solution.py:201
  625.6 1.8 multiply_convert_fusion
  (55 shorter events, 4.6 us)
Async XLA Ops:
  2.6 34.2 %all-to-all-start.1 = ((bf16[1,32,2]{2,0,1:T(2,128)(2,1)}), bf16[1,32,2]{2,0,1:T(2,128)(2,1)S(1)}, u32[]{:S(2)}, u32[]{:S(2)}) async-start(bf16[1,32,2]{2,0,1:T(2,128)(2,1)} %convert_element_type.186), calls=%async_computation.1 | async-start | bytes 32768 | tf_op jit(solution)/shard_map/all_to_all | solution.py:69
  36.8 12.3 %copy-start.3 = (s32[512]{0:T(512)S(1)}, s32[512]{0:T(512)}, u32[]{:S(2)}) copy-start(s32[512]{0:T(512)} %param.11) | copy-start | bytes 6148
  36.8 14.5 %copy-start.1 = (f32[3,7,256]{2,1,0:T(8,128)S(1)}, f32[3,7,256]{2,1,0:T(8,128)}, u32[]{:S(2)}) copy-start(f32[3,7,256]{2,1,0:T(8,128)} %param.12) | copy-start | bytes 64516
  36.8 14.5 %copy-start.2 = (bf16[16,512]{1,0:T(8,128)(2,1)S(1)}, bf16[16,512]{1,0:T(8,128)(2,1)}, u32[]{:S(2)}) copy-start(bf16[16,512]{1,0:T(8,128)(2,1)} %param.13) | copy-start | bytes 49156
  36.8 157.5 %all-to-all-start = ((bf16[3,32,2,8192]{3,2,0,1:T(2,128)(2,1)}), bf16[3,32,2,8192]{3,2,0,1:T(2,128)(2,1)S(1)}, u32[]{:S(2)}, u32[]{:S(2)}) async-start(bf16[3,32,2,8192]{3,2,0,1:T(2,128)(2,1)} %copy.32), calls=%async_computation | async-start | bytes 6291456 | tf_op jit(solution)/shard_map/all_to_all | solution.py:62
  49.3 129.8 %collective-permute-start = (f32[6]{0:T(128)S(1)}, f32[6]{0:T(128)S(1)}, u32[]{:S(2)}, u32[]{:S(2)}) collective-permute-start(f32[6]{0:T(128)S(1)} %slice.98), channel_id=1, source_target_pairs={{0,16},{16,32},{32,48},{48,64},{64,80},{80,96},{96,112},{112,128},... | collective-permute-start | bytes 80 | tf_op jit(solution)/shard_map/ppermute | solution.py:18
  194.4 24.2 %all-to-all-start.4 = ((bf16[32,2,128]{2,1,0:T(2,128)(2,1)}), bf16[32,2,128]{2,1,0:T(2,128)(2,1)S(1)}, u32[]{:S(2)}, u32[]{:S(2)}) async-start(bf16[32,2,128]{2,1,0:T(2,128)(2,1)} %reshape.263), calls=%async_computation.4 | async-start | bytes 32768 | tf_op jit(solution)/shard_map/all_to_all | solution.py:100
  209.4 5.0 collective-permute-start.1
  216.6 1.2 copy-start
  218.6 34.3 %all-to-all-start.2 = ((bf16[32,16,256]{2,1,0:T(8,128)(2,1)}), bf16[32,16,256]{2,1,0:T(8,128)(2,1)S(1)}, u32[]{:S(2)}, u32[]{:S(2)}) async-start(bf16[32,16,256]{2,1,0:T(8,128)(2,1)} %bitcast.9), calls=%async_computation.2 | async-start | bytes 524288 | tf_op jit(solution)/shard_map/all_to_all | solution.py:93
  252.8 21.6 %all-to-all-start.5 = ((f32[32,1,1024]{2,1,0:T(1,128)}), f32[32,1,1024]{2,1,0:T(1,128)S(1)}, u32[]{:S(2)}, u32[]{:S(2)}) async-start(f32[32,1,1024]{2,1,0:T(1,128)} %reshape.265), calls=%async_computation.5 | async-start | bytes 262144 | tf_op jit(solution)/shard_map/all_to_all | solution.py:129
  274.5 105.2 %all-to-all-start.3 = ((f32[2,32,2,16,256]{4,3,2,0,1:T(8,128)}), f32[2,32,2,16,256]{4,3,2,0,1:T(8,128)S(1)}, u32[]{:S(2)}, u32[]{:S(2)}) async-start(f32[2,32,2,16,256]{4,3,2,0,1:T(8,128)} %pad_maximum_fusion), calls=%async_computation.3 | async-start | bytes 4194304 | tf_op jit(solution)/shard_map/all_to_all | solution.py:128
  544.1 39.7 %copy-start.4 = (f32[256]{0:T(256)S(1)}, f32[256]{0:T(256)}, u32[]{:S(2)}) copy-start(f32[256]{0:T(256)} %param.14) | copy-start | bytes 3076
  545.2 80.4 %copy-start.5 = (f32[256]{0:T(256)S(1)}, f32[256]{0:T(256)}, u32[]{:S(2)}) copy-start(f32[256]{0:T(256)} %param.15) | copy-start | bytes 3076
  545.2 38.6 %all-to-all-start.7 = ((f32[32,16,256]{2,1,0:T(8,128)}), f32[32,16,256]{2,1,0:T(8,128)S(1)}, u32[]{:S(2)}, u32[]{:S(2)}) async-start(f32[32,16,256]{2,1,0:T(8,128)} %copy.57), calls=%async_computation.7 | async-start | bytes 1048576 | tf_op jit(solution)/shard_map/all_to_all | solution.py:162
where the time goes:
time: 637 us; the launch traced here: 628 us
  waiting for transfers between devices  279 us (44%)
  blocking collectives  144 us (23%)
  matrix products  86.5 us (14%)
  starting transfers between devices  65.6 us (10%)
  local copies, waits for them, and re-layouts  40.5 us (6%)
  other arithmetic  10.4 us (2%)
    ppermute x2, waiting for transfers between devices, from_behind(): return lax.ppermute(block, axis, route)  130 us
    all_to_all x1, blocking collectives, sequence_conv(): lax.all_to_all(stacked, 'seq', split_axis=2, concat_axis=1, tiled=True)  103 us
    dot_general x16, matrix products, contract(): return jnp.einsum(einsum_form, left_side, right_side, precision=highest)  82 us
    all_to_all x1, waiting for transfers between devices, sequence_conv(): lax.all_to_all(forward_outer(signal), 'seq', split_axis=1, concat_axis=3,...  73.4 us
    psum x1, blocking collectives, local(): lax.psum(jnp.sum(gated_rows * gated_rows, axis=1), 'chan') / CHANNELS  40.7 us
    all_to_all x1, waiting for transfers between devices, sequence_conv(): lax.all_to_all(result, 'seq', split_axis=0, concat_axis=1, tiled=True)  31 us
    all_to_all x1, waiting for transfers between devices, sequence_conv(): lax.all_to_all(mixed_rows.reshape(devices, block_rows, chans_here), 'seq'...  18.2 us
    all_to_all x1, starting transfers between devices, arrange_tiles(): lax.all_to_all(labels.reshape(1, devices, per_pair), 'seq', split_axis=1,...  15.4 us
  transfers between devices with their start and end apart: 9, of which 7 were waited for; matrix products, arithmetic and copies ran while one was open for 11% of the time, Pallas kernels for 0%

commit v1 on v0

v1 whole, which is shorter than its diff:
```python
import functools

import jax
import jax.numpy as jnp
from jax import lax
from jax.experimental import pallas as pl
from jax.experimental.pallas import tpu as pltpu
from jax.sharding import PartitionSpec as P

TILE = 32
LANES = 128
TAPS = 7
f32 = jnp.float32
bf16 = jnp.bfloat16


def vmem(mib):
    return pltpu.CompilerParams(vmem_limit_bytes=mib << 20)


def turned(block):
    return jnp.transpose(block.astype(f32)).reshape(32, 8, LANES)


def pack_qk_kernel(rows_ref, extra_ref, out_ref):
    step = pl.program_id(0)

    @pl.when(step < 8)
    def _():
        both = jnp.concatenate([turned(rows_ref[0]), turned(rows_ref[1])], axis=1)
        out_ref[:, 0] = both.astype(bf16)

    @pl.when(step == 8)
    def _():
        out_ref[:, 0] = extra_ref[...]


def pack_qk(loaded, extra):
    return pl.pallas_call(
        pack_qk_kernel,
        grid=(9,),
        in_specs=[
            pl.BlockSpec((2, LANES, 256), lambda i: (0, jnp.minimum(i, 7), 0)),
            pl.BlockSpec((32, 16, LANES), lambda i: (0, 0, 0)),
        ],
        out_specs=pl.BlockSpec((32, 1, 16, LANES), lambda i: (0, i, 0, 0)),
        out_shape=jax.ShapeDtypeStruct((32, 9, 16, LANES), bf16),
        compiler_params=vmem(8),
        name="pack_qk",
    )(loaded, extra)


def pack_v_kernel(rows_ref, out_ref):
    both = jnp.concatenate(
        [turned(rows_ref[0, :LANES]), turned(rows_ref[0, LANES:])], axis=1
    )
    out_ref[:, 0] = both.astype(bf16)


def pack_v(loaded):
    return pl.pallas_call(
        pack_v_kernel,
        grid=(4,),
        in_specs=[pl.BlockSpec((1, 2 * LANES, 256), lambda i: (2, i, 0))],
        out_specs=pl.BlockSpec((32, 1, 16, LANES), lambda i: (0, i, 0, 0)),
        out_shape=jax.ShapeDtypeStruct((32, 4, 16, LANES), bf16),
        compiler_params=vmem(8),
        name="pack_v",
    )(loaded)


def gathered_column(table_ref, column, group, fetch):
    out = None
    for b in range(4):
        src = table_ref[column * 4 + b]
        tile = pltpu.roll(fetch(src), ((b - src) & 3) * TILE, 1)
        out = tile if out is None else jnp.where(group == b, tile, out)
    return out


def short_conv(block, before, reach, taps_ref, lane):
    rolled = [pltpu.roll(block, j, 1) for j in range(1, TAPS)]
    total = block * taps_ref[0]
    for j in range(1, TAPS):
        delayed = jnp.where(lane >= j, rolled[j - 1], before[j - 1])
        total = total + jnp.where(reach >= j, delayed, 0.0) * taps_ref[j]
    return total, rolled


def qk_kernel(table_ref, recv_ref, reach_ref, taps_ref, gate_ref, key_ref):
    lane = lax.broadcasted_iota(jnp.int32, (16, LANES), 1)
    group = lane // TILE

    def fetch(src):
        return recv_ref[src >> 5, (src >> 2) & 7].astype(f32)

    def step(column, before):
        block = gathered_column(table_ref, column, group, fetch)
        reach = jnp.broadcast_to(reach_ref[pl.ds(column, 1), :], (16, LANES))
        done, rolled = short_conv(block, before, reach, taps_ref, lane)
        gate_ref[column] = done[:8].astype(bf16).astype(f32)
        key_ref[column] = done[8:]
        return rolled

    zero = [jnp.zeros((16, LANES), f32)] * (TAPS - 1)
    lax.fori_loop(0, LANES, step, zero, unroll=2)


def qk_rows(table, recv, reach, taps):
    whole = pl.BlockSpec(memory_space=pltpu.VMEM)
    return pl.pallas_call(
        qk_kernel,
        in_specs=[pl.BlockSpec(memory_space=pltpu.SMEM), whole, whole, whole],
        out_specs=[whole, whole],
        out_shape=[jax.ShapeDtypeStruct((LANES, 8, LANES), f32)] * 2,
        compiler_params=vmem(8),
        name="qk_rows",
    )(table, recv, reach, taps)


def blocks_kernel(meta_ref, out_ref, lags_ref):
    lags_ref[...] = meta_ref[:, 0].astype(f32)
    row = lax.broadcasted_iota(jnp.int32, (LANES, LANES), 0)
    col = lax.broadcasted_iota(jnp.int32, (LANES, LANES), 1)
    upper = col >= row

    def step(f, before):
        for k in range(4):
            line = jnp.broadcast_to(lags_ref[f, k : k + 1, :], (LANES, LANES))
            skew = pltpu.roll(line, 0, 1, stride=1, stride_axis=0)
            block = jnp.where(upper, skew, before).astype(bf16)
            if k == 0:
                out_ref[f, 0:128, 0:128] = block
                out_ref[f, 128:256, 128:256] = block
            elif k == 1:
                out_ref[f, 0:128, 128:256] = block
                out_ref[f, 384:512, 0:128] = block
            elif k == 2:
                out_ref[f, 256:384, 0:128] = block
                out_ref[f, 384:512, 128:256] = block
            else:
                out_ref[f, 256:384, 128:256] = block

                @pl.when(f < 31)
                def _():
                    out_ref[f + 1, 128:256, 0:128] = block

            before = skew
        return before

    out_ref[0, 128:256, 0:128] = jnp.zeros((LANES, LANES), bf16)
    lax.fori_loop(0, 32, step, jnp.zeros((LANES, LANES), f32))


def toeplitz_blocks(recv):
    return pl.pallas_call(
        blocks_kernel,
        grid=(1,),
        in_specs=[pl.BlockSpec((32, 1, 16, LANES), lambda i: (0, 8, 0, 0))],
        out_specs=pl.BlockSpec((32, 512, 256), lambda i: (0, 0, 0), pipeline_mode=pl.Buffered(1)),
        out_shape=jax.ShapeDtypeStruct((32, 512, 256), bf16),
        scratch_shapes=[pltpu.VMEM((32, 16, LANES), f32)],
        compiler_params=vmem(14),
        name="toeplitz_blocks",
    )(recv)


def conv_kernel(
    table_ref, recv_ref, reach_ref, taps_ref, skip_ref, gate_ref, key_ref, blocks_ref,
    out_ref, rows_ref, acc_ref,
):
    lane = lax.broadcasted_iota(jnp.int32, (8, LANES), 1)
    group = lane // TILE
    rows_ref[0:128, :] = jnp.zeros((128, 512), bf16)

    def fetch(src):
        pair = recv_ref[src >> 5, (src >> 3) & 3].astype(f32)
        return jnp.where(((src >> 2) & 1) == 1, pair[8:], pair[:8])

    def place(u, carry):
        before, last = carry
        mixed = []
        for k in range(4):
            column = 4 * u + k
            block = gathered_column(table_ref, column, group, fetch)
            reach = jnp.broadcast_to(reach_ref[pl.ds(column, 1), :], (8, LANES))
            done, before = short_conv(block, before, reach, taps_ref, lane)
            mixed.append(done * key_ref[column])
        first = jnp.concatenate(mixed[:2], axis=1)
        second = jnp.concatenate(mixed[2:], axis=1)
        at = pl.ds(pl.multiple_of(128 + 16 * u, 16), 16)
        rows_ref[at, 0:256] = jnp.concatenate([first, second], axis=0).astype(bf16)
        rows_ref[at, 256:512] = jnp.concatenate([last, first], axis=0).astype(bf16)
        return before, second

    zero = [jnp.zeros((8, LANES), f32)] * (TAPS - 1)
    lax.fori_loop(0, 32, place, (zero, jnp.zeros((8, 256), f32)))

    for part in range(4):
        begin = 128 * part
        count = 512 - begin

        def multiply(f, carry, begin=begin, count=count, part=part):
            at = pl.multiple_of(128 + begin - 16 * f, 16)
            product = jnp.dot(
                rows_ref[pl.ds(at, count), :], blocks_ref[f], preferred_element_type=f32
            )
            if part == 0:

                @pl.when(f == 0)
                def _():
                    acc_ref[...] = product

                @pl.when(f > 0)
                def _():
                    acc_ref[...] += product

            else:
                acc_ref[begin:, :] += product
            return carry

        lax.fori_loop(8 * part, 8 * part + 8, multiply, 0)

    skip = jnp.broadcast_to(skip_ref[...], (16, 256))

    def finish(u, carry):
        at = pl.ds(pl.multiple_of(16 * u, 16), 16)
        here = pl.ds(pl.multiple_of(128 + 16 * u, 16), 16)
        total = acc_ref[at, :] + skip * rows_ref[here, 0:256].astype(f32)
        first = jnp.concatenate([gate_ref[4 * u], gate_ref[4 * u + 1]], axis=1)
        second = jnp.concatenate([gate_ref[4 * u + 2], gate_ref[4 * u + 3]], axis=1)
        out_ref[u] = (jnp.concatenate([first, second], axis=0) * total).astype(bf16)
        return carry

    lax.fori_loop(0, 32, finish, 0, unroll=2)


def conv_rows(table, recv, reach, taps, skip, gate, key, blocks):
    whole = pl.BlockSpec(memory_space=pltpu.VMEM)
    return pl.pallas_call(
        conv_kernel,
        in_specs=[pl.BlockSpec(memory_space=pltpu.SMEM)] + [whole] * 7,
        out_specs=whole,
        out_shape=jax.ShapeDtypeStruct((32, 16, 256), bf16),
        scratch_shapes=[pltpu.VMEM((640, 512), bf16), pltpu.VMEM((512, 256), f32)],
        compiler_params=vmem(20),
        name="conv_rows",
    )(table, recv, reach, taps, skip, gate, key, blocks)


def power_kernel(in_ref, out_ref):
    for half in range(2):
        block = in_ref[:, 8 * half : 8 * half + 8, :].astype(f32).reshape(256, 256)
        out_ref[half : half + 1, :] = jnp.sum(block * block, axis=0, keepdims=True)


def power_rows(rows):
    return pl.pallas_call(
        power_kernel,
        out_shape=jax.ShapeDtypeStruct((2, 256), f32),
        compiler_params=vmem(4),
        name="power_rows",
    )(rows)


def turn_kernel(in_ref, out_ref):
    for half in range(2):
        block = in_ref[:, 8 * half : 8 * half + 8, :].astype(f32).reshape(256, 256)
        out_ref[256 * half : 256 * half + 256, :] = jnp.transpose(block).astype(bf16)


def turn_rows(rows):
    return pl.pallas_call(
        turn_kernel,
        out_shape=jax.ShapeDtypeStruct((512, 256), bf16),
        compiler_params=vmem(4),
        name="turn_rows",
    )(rows)


def exchange(block, axis):
    return lax.all_to_all(block, axis, split_axis=0, concat_axis=0, tiled=True)


def local(
    loaded, dest_tiles, tile_counts, segments, short_filters, long_filters, skip_gain, norm_gain
):
    position = lax.axis_index("seq")
    lags = jnp.repeat(long_filters.reshape(16, 4, LANES), 2, axis=0)
    seg_part = jnp.broadcast_to(segments.reshape(1, 4, LANES), (32, 4, LANES)).astype(bf16)
    slots = jnp.concatenate(
        [dest_tiles // 16, dest_tiles % 16, tile_counts, jnp.zeros((63,), jnp.int32)]
    )
    slot_part = jnp.broadcast_to(slots.reshape(1, 1, LANES), (32, 1, LANES)).astype(bf16)
    extra = jnp.concatenate(
        [lags, seg_part, slot_part, jnp.zeros((32, 7, LANES), bf16)], axis=1
    )

    recv_qk = exchange(pack_qk(loaded, extra), "seq")
    recv_v = exchange(pack_v(loaded), "seq")

    known = recv_qk[:, 8].astype(f32).astype(jnp.int32)
    seg = known[:, 4:8].reshape(-1)
    placed = known[:, 8, 0:32] * 16 + known[:, 8, 32:64]
    used = jnp.arange(32, dtype=jnp.int32)[None, :] < known[:, 8, 64:65]
    placed = jnp.where(used, placed, -1).reshape(-1)
    tiles = jnp.arange(512, dtype=jnp.int32)
    slot_ids = jnp.arange(1024, dtype=jnp.int32)
    table = jnp.sum(
        jnp.where(placed[None, :] == tiles[:, None], slot_ids[None, :], 0), axis=1
    ).astype(jnp.int32)
    reach = jnp.zeros(seg.shape, jnp.int32)
    for j in range(1, TAPS):
        reach = reach + jnp.concatenate(
            [jnp.zeros((j,), jnp.int32), (seg[j:] == seg[:-j]).astype(jnp.int32)]
        )
    reach = reach.reshape(LANES, LANES)

    taps = lax.dynamic_slice_in_dim(short_filters, position * 8, 8, 2)
    taps = jnp.broadcast_to(taps[..., None], (3, TAPS, 8, LANES))
    taps_qk = jnp.transpose(taps[:2], (1, 0, 2, 3)).reshape(TAPS, 16, LANES)
    skip = lax.dynamic_slice_in_dim(skip_gain, position * 8, 8, 0)
    skip = jnp.tile(skip, 2)[:, None]

    gate, key = qk_rows(table, recv_qk, reach, taps_qk)
    blocks = toeplitz_blocks(recv_qk)
    gated = conv_rows(table, recv_v, reach, taps[2], skip, gate, key, blocks)
    mine = exchange(gated, "seq")
    power = power_rows(mine).reshape(-1)
    every = exchange(jnp.broadcast_to(power[None], (16, 512)), "chan")
    scale = lax.rsqrt(jnp.sum(every, axis=0) / 4096.0 + 1e-06)
    rows = turn_rows(mine)
    return (rows.astype(f32) * scale[:, None] * norm_gain[None, :]).astype(bf16)


def solution(mesh):
    return jax.shard_map(
        local,
        mesh=mesh,
        in_specs=(
            P(None, "seq", "chan"),
            P("seq"),
            P("seq"),
            P("seq"),
            P(None, None, "chan"),
            P("chan", "seq"),
            P("chan"),
            P("chan"),
        ),
        out_specs=P("seq", "chan"),
        check_vma=False,
    )
```

time: 637 us -> 183 us (0.29)
  the two profiles are of different devices: /device:TPU:32 before, /device:TPU:1 now
where the time goes in v1:
time: 183 us; the launch traced here: 182 us
  waiting for transfers between devices  77.3 us (42%)
  Pallas kernels  35.5 us (19%)
  starting transfers between devices  27.7 us (15%)
  blocking collectives  25.4 us (14%)
  local copies, waits for them, and re-layouts  11.9 us (7%)
  other arithmetic  3.63 us (2%)
    all_to_all x3, waiting for transfers between devices, exchange(): return lax.all_to_all(block, axis, split_axis=0, concat_axis=0, tiled=True)  77.3 us
    all_to_all x3, starting transfers between devices, exchange(): return lax.all_to_all(block, axis, split_axis=0, concat_axis=0, tiled=True)  27.7 us
    all_to_all x1, blocking collectives, exchange(): return lax.all_to_all(block, axis, split_axis=0, concat_axis=0, tiled=True)  25.4 us
    pallas_call x1, Pallas kernels, conv_rows(): pl.pallas_call(conv_kernel, in_specs=[pl.BlockSpec(memory_space=pltpu.SME...  16.1 us
    pallas_call x1, Pallas kernels, qk_rows(): pl.pallas_call(qk_kernel, in_specs=[pl.BlockSpec(memory_space=pltpu.SMEM)...  12.4 us
    unnamed x17, local copies, waits for them, and re-layouts  9.03 us
    pallas_call x1, Pallas kernels, toeplitz_blocks(): pl.pallas_call(blocks_kernel, grid=(1,), in_specs=[pl.BlockSpec((32, 1, 1...  3.95 us
  transfers between devices with their start and end apart: 3, of which 3 were waited for; matrix products, arithmetic and copies ran while one was open for 1% of the time, Pallas kernels for 10%

profile of v1, /device:TPU:1, one launch (start us, length us, event | category | flops | bytes accessed | tf_op | source)
XLA Modules:
  0.0 182.3 jit_solution(16229991731198889035)
XLA Ops:
  0.0 0.0 copy-start
  0.0 0.7 fusion.2
  1.3 0.7 reshape.86
  2.1 0.7 convert_bitcast_fusion.1
  2.8 0.1 pad.15.clone
  2.8 0.1 pad_maximum_fusion
  3.0 0.1 maximum_maximum_fusion.extra_ref
  3.1 0.0 copy-start.3
  3.1 1.4 copy-done.3
  4.5 0.0 copy-start.4
  4.5 1.2 pack_qk.1
  5.7 0.0 copy-start.5
  5.7 1.0 copy-done.5
  6.7 0.0 copy-start.7
  6.7 16.9 %all-to-all-start = ((bf16[32,9,16,128]{3,2,1,0:T(8,128)(2,1)}), bf16[32,9,16,128]{3,2,1,0:T(8,128)(2,1)S(1)}, u32[]{:S(2)}, u32[]{:S(2)}) async-start(bf16[32,9,16,128]{3,2,1,0:T(8,128)(2,1)} %copy-done.5), calls=%async_computation | async-start | bytes 2359296 | tf_op jit(solution)/shard_map/all_to_all | solution.py:282
  23.6 0.0 copy-done.4
  23.6 1.7 pack_v.1
  25.3 0.0 copy-done
  25.3 0.1 constant_dynamic-slice_fusion
  25.4 0.0 copy-done.7
  25.4 0.1 dynamic_slice.7
  25.5 0.1 broadcast_in_dim_tile.4.skip_ref
  25.6 0.1 dynamic-slice_bitcast_fusion
  25.6 0.1 broadcast_bitcast_fusion.taps_ref
  25.7 59.2 %all-to-all-done.recv_ref.meta_ref = bf16[32,9,16,128]{3,2,1,0:T(8,128)(2,1)S(1)} async-done(((bf16[32,9,16,128]{3,2,1,0:T(8,128)(2,1)}), bf16[32,9,16,128]{3,2,1,0:T(8,128)(2,1)S(1)}, u32[]{:S(2)}, u32[]{:S(2)}) %all-to-all-start) | async-done | bytes 1179680 | tf_op jit(solution)/shard_map/all_to_all | solution.py:282
  84.9 4.0 %all-to-all-start.1 = ((bf16[32,4,16,128]{3,2,1,0:T(8,128)(2,1)}), bf16[32,4,16,128]{3,2,1,0:T(8,128)(2,1)S(1)}, u32[]{:S(2)}, u32[]{:S(2)}) async-start(bf16[32,4,16,128]{3,2,1,0:T(8,128)(2,1)} %pack_v.1), calls=%async_computation.1 | async-start | bytes 1048576 | tf_op jit(solution)/shard_map/all_to_all | solution.py:282
  89.0 0.1 slice_compare_fusion
  89.1 0.1 slice_compare_fusion.1
  89.2 0.1 slice_compare_fusion.2
  89.3 0.1 fusion
  89.4 0.7 slice_reduce_fusion
  90.1 0.1 add.48
  90.2 0.1 iota_compare_fusion.1
  90.3 0.1 lt.37
  90.4 4.0 %toeplitz_blocks.1.blocks_ref = bf16[32,512,256]{2,1,0:T(8,128)(2,1)S(1)} custom-call(bf16[32,9,16,128]{3,2,1,0:T(8,128)(2,1)S(1)} %all-to-all-done.recv_ref.meta_ref), custom_call_target="tpu_custom_call" | custom-call | tf_op jit(solution)/shard_map/toeplitz_blocks/pallas_call | solution.py:156
  94.3 0.0 copy-start.1
  94.3 3.2 %copy-done.1 = bf16[32,512,256]{2,1,0:T(8,128)(2,1)} copy-done((bf16[32,512,256]{2,1,0:T(8,128)(2,1)}, bf16[32,512,256]{2,1,0:T(8,128)(2,1)S(1)}, u32[]{:S(2)}) %copy-start.1) | copy-done | bytes 8388632
  97.5 0.1 slice_compare_fusion.3
  97.6 0.1 slice_compare_fusion.4
  97.7 0.1 slice_compare_fusion.5
  97.8 0.2 add_bitcast_fusion.reach_ref
  98.0 0.3 select_reduce_fusion.table_ref
  98.3 12.4 %qk_rows.1 = (f32[128,8,128]{2,1,0:T(8,128)S(1)}, f32[128,8,128]{2,1,0:T(8,128)S(1)}) custom-call(s32[512]{0:T(512)S(1)} %select_reduce_fusion.table_ref, bf16[32,9,16,128]{3,2,1,0:T(8,128)(2,1)S(1)} %all-to-all-done.recv_ref.meta_ref, s32[128,128]{1,0:T(8,128)S(1)} %add_bitcast_fusion.reach_ref, f32[7,16,128]{2,1,0:T(8,128)S(1)} %broadcast_bitcast_fusion.taps_ref), custom_call_target="tpu_custom_call" | custom-call | tf_op jit(solution)/shard_map/qk_rows/pallas_call | solution.py:111
  110.7 11.8 %all-to-all-done.1.recv_ref = bf16[32,4,16,128]{3,2,1,0:T(8,128)(2,1)S(1)} async-done(((bf16[32,4,16,128]{3,2,1,0:T(8,128)(2,1)}), bf16[32,4,16,128]{3,2,1,0:T(8,128)(2,1)S(1)}, u32[]{:S(2)}, u32[]{:S(2)}) %all-to-all-start.1) | async-done | bytes 524320 | tf_op jit(solution)/shard_map/all_to_all | solution.py:282
  122.5 0.1 broadcast_in_dim.66.taps_ref
  122.6 0.0 copy-start.2
  122.6 3.4 %copy-done.2 = bf16[32,512,256]{2,1,0:T(8,128)(2,1)S(1)} copy-done((bf16[32,512,256]{2,1,0:T(8,128)(2,1)S(1)}, bf16[32,512,256]{2,1,0:T(8,128)(2,1)}, u32[]{:S(2)}) %copy-start.2) | copy-done | bytes 8388632
  125.9 0.0 copy-start.6
  125.9 16.1 %conv_rows.1 = bf16[32,16,256]{2,1,0:T(8,128)(2,1)S(1)} custom-call(s32[512]{0:T(512)S(1)} %select_reduce_fusion.table_ref, bf16[32,4,16,128]{3,2,1,0:T(8,128)(2,1)S(1)} %all-to-all-done.1.recv_ref, s32[128,128]{1,0:T(8,128)S(1)} %add_bitcast_fusion.reach_ref, f32[7,8,128]{2,1,0:T(8,128)S(1)} %broadcast_in_dim.66.taps_ref, ...), custom_call_target="tpu_custom_call" | custom-call | tf_op jit(solution)/shard_map/conv_rows/pallas_call | solution.py:240
  142.0 25.4 %all_to_all.21.in_ref = bf16[32,16,256]{2,1,0:T(8,128)(2,1)S(1)} all-to-all(bf16[32,16,256]{2,1,0:T(8,128)(2,1)S(1)} %conv_rows.1), channel_id=1, replica_groups=mesh['seq'=32,'chan'=16] {'seq'}, dimensions={0} | all-to-all | bytes 524288 | tf_op jit(solution)/shard_map/all_to_all | solution.py:282
  167.5 0.6 broadcast_in_dim.69
  168.1 6.8 %all-to-all-start.3 = ((f32[16,1,512]{2,1,0:T(1,128)}), f32[16,1,512]{2,1,0:T(1,128)S(1)}, u32[]{:S(2)}, u32[]{:S(2)}) async-start(f32[16,1,512]{2,1,0:T(1,128)} %broadcast_in_dim.69), calls=%async_computation.3 | async-start | bytes 65536 | tf_op jit(solution)/shard_map/all_to_all | solution.py:282
  174.9 0.1 turn_rows.1
  175.0 6.3 %all-to-all-done.3 = f32[16,1,512]{2,1,0:T(1,128)S(1)} async-done(((f32[16,1,512]{2,1,0:T(1,128)}), f32[16,1,512]{2,1,0:T(1,128)S(1)}, u32[]{:S(2)}, u32[]{:S(2)}) %all-to-all-start.3) | async-done | bytes 32800 | tf_op jit(solution)/shard_map/all_to_all | solution.py:282
  181.4 0.0 copy-done.6
  181.4 0.8 multiply_convert_fusion
  (14 shorter events, 0.2 us)
Async XLA Ops:
  0.0 25.3 %copy-start = (f32[3,7,256]{2,1,0:T(8,128)S(1)}, f32[3,7,256]{2,1,0:T(8,128)}, u32[]{:S(2)}) copy-start(f32[3,7,256]{2,1,0:T(8,128)} %param.12) | copy-start | bytes 64516
  3.1 1.4 copy-start.3
  4.5 19.1 %copy-start.4 = (bf16[3,1024,256]{2,1,0:T(8,128)(2,1)S(1)}, bf16[3,1024,256]{2,1,0:T(8,128)(2,1)}, u32[]{:S(2)}) copy-start(bf16[3,1024,256]{2,1,0:T(8,128)(2,1)} %rows_ref.3) | copy-start | bytes 4718596
  5.7 1.0 copy-start.5
  6.7 18.7 %copy-start.7 = (f32[256]{0:T(256)S(1)}, f32[256]{0:T(256)}, u32[]{:S(2)}) copy-start(f32[256]{0:T(256)} %param.14) | copy-start | bytes 3076
  6.7 78.2 %all-to-all-start = ((bf16[32,9,16,128]{3,2,1,0:T(8,128)(2,1)}), bf16[32,9,16,128]{3,2,1,0:T(8,128)(2,1)S(1)}, u32[]{:S(2)}, u32[]{:S(2)}) async-start(bf16[32,9,16,128]{3,2,1,0:T(8,128)(2,1)} %copy-done.5), calls=%async_computation | async-start | bytes 2359296 | tf_op jit(solution)/shard_map/all_to_all | solution.py:282
  84.9 37.6 %all-to-all-start.1 = ((bf16[32,4,16,128]{3,2,1,0:T(8,128)(2,1)}), bf16[32,4,16,128]{3,2,1,0:T(8,128)(2,1)S(1)}, u32[]{:S(2)}, u32[]{:S(2)}) async-start(bf16[32,4,16,128]{3,2,1,0:T(8,128)(2,1)} %pack_v.1), calls=%async_computation.1 | async-start | bytes 1048576 | tf_op jit(solution)/shard_map/all_to_all | solution.py:282
  94.3 3.2 %copy-start.1 = (bf16[32,512,256]{2,1,0:T(8,128)(2,1)}, bf16[32,512,256]{2,1,0:T(8,128)(2,1)S(1)}, u32[]{:S(2)}) copy-start(bf16[32,512,256]{2,1,0:T(8,128)(2,1)S(1)} %toeplitz_blocks.1.blocks_ref) | copy-start | bytes 25165828
  122.6 3.4 %copy-start.2 = (bf16[32,512,256]{2,1,0:T(8,128)(2,1)S(1)}, bf16[32,512,256]{2,1,0:T(8,128)(2,1)}, u32[]{:S(2)}) copy-start(bf16[32,512,256]{2,1,0:T(8,128)(2,1)} %copy-done.1) | copy-start | bytes 25165828
  125.9 55.5 %copy-start.6 = (f32[256]{0:T(256)S(1)}, f32[256]{0:T(256)}, u32[]{:S(2)}) copy-start(f32[256]{0:T(256)} %param.15) | copy-start | bytes 3076
  168.1 13.2 %all-to-all-start.3 = ((f32[16,1,512]{2,1,0:T(1,128)}), f32[16,1,512]{2,1,0:T(1,128)S(1)}, u32[]{:S(2)}, u32[]{:S(2)}) async-start(f32[16,1,512]{2,1,0:T(1,128)} %broadcast_in_dim.69), calls=%async_computation.3 | async-start | bytes 65536 | tf_op jit(solution)/shard_map/all_to_all | solution.py:282

commit v2 on v1

v2 whole, which is shorter than its diff:
```python
import functools

import jax
import jax.numpy as jnp
from jax import lax
from jax.experimental import pallas as pl
from jax.experimental.pallas import tpu as pltpu
from jax.sharding import PartitionSpec as P

TILE = 32
LANES = 128
TAPS = 7
f32 = jnp.float32
bf16 = jnp.bfloat16


def vmem(mib):
    return pltpu.CompilerParams(vmem_limit_bytes=mib << 20)


def turned(block):
    return jnp.transpose(block.astype(f32)).reshape(32, 8, LANES)


def pack_kernel(rows_ref, out_ref):
    out_ref[:, 0] = jnp.concatenate([turned(rows_ref[t]) for t in range(3)], axis=1).astype(bf16)


def pack(loaded):
    return pl.pallas_call(
        pack_kernel,
        grid=(8,),
        in_specs=[pl.BlockSpec((3, LANES, 256), lambda i: (0, i, 0))],
        out_specs=pl.BlockSpec((32, 1, 24, LANES), lambda i: (0, i, 0, 0)),
        out_shape=jax.ShapeDtypeStruct((32, 8, 24, LANES), bf16),
        compiler_params=vmem(8),
        name="pack",
    )(loaded)


def blocks_kernel(lags_ref, out_ref):
    row = lax.broadcasted_iota(jnp.int32, (LANES, LANES), 0)
    col = lax.broadcasted_iota(jnp.int32, (LANES, LANES), 1)
    upper = col >= row

    def step(f, before):
        for k in range(8):
            line = jnp.broadcast_to(lags_ref[8 * f + k, :, :], (LANES, LANES))
            skew = pltpu.roll(line, 0, 1, stride=1, stride_axis=0)
            out_ref[8 * f + k + 1] = jnp.where(upper, skew, before).astype(bf16)
            before = skew
        return before

    out_ref[0] = jnp.zeros((LANES, LANES), bf16)
    lax.fori_loop(0, 16, step, jnp.zeros((LANES, LANES), f32))


def toeplitz_blocks(lags):
    whole = pl.BlockSpec(memory_space=pltpu.VMEM)
    return pl.pallas_call(
        blocks_kernel,
        in_specs=[whole],
        out_specs=whole,
        out_shape=jax.ShapeDtypeStruct((129, LANES, LANES), bf16),
        compiler_params=vmem(8),
        name="toeplitz_blocks",
    )(lags)


def gathered_column(table_ref, recv_ref, column, group):
    out = None
    for b in range(4):
        src = table_ref[column * 4 + b]
        tile = recv_ref[src >> 5, (src >> 2) & 7].astype(f32)
        tile = pltpu.roll(tile, ((b - src) & 3) * TILE, 1)
        out = tile if out is None else jnp.where(group == b, tile, out)
    return out


def conv_kernel(
    table_ref, recv_ref, reach_ref, taps_ref, skip_ref, lags_ref, out_ref,
    rows_ref, acc_ref, gate_ref, blocks_ref, sem,
):
    fetch = pltpu.make_async_copy(lags_ref, blocks_ref, sem)
    fetch.start()
    lane = lax.broadcasted_iota(jnp.int32, (24, LANES), 1)
    group = lane // TILE
    rows_ref[0:128, :] = jnp.zeros((128, 512), bf16)

    def place(u, carry):
        before, last = carry
        mixed = []
        gates = []
        for k in range(4):
            column = 4 * u + k
            block = gathered_column(table_ref, recv_ref, column, group)
            reach = jnp.broadcast_to(reach_ref[pl.ds(column, 1), :], (24, LANES))
            rolled = [pltpu.roll(block, j, 1) for j in range(1, TAPS)]
            total = block * taps_ref[0]
            for j in range(1, TAPS):
                delayed = jnp.where(lane >= j, rolled[j - 1], before[j - 1])
                total = total + jnp.where(reach >= j, delayed, 0.0) * taps_ref[j]
            before = rolled
            gates.append(total[:8])
            mixed.append(total[8:16] * total[16:])
        first = jnp.concatenate(mixed[:2], axis=1)
        second = jnp.concatenate(mixed[2:], axis=1)
        at = pl.ds(pl.multiple_of(128 + 16 * u, 16), 16)
        rows_ref[at, 0:256] = jnp.concatenate([first, second], axis=0).astype(bf16)
        rows_ref[at, 256:512] = jnp.concatenate([last, first], axis=0).astype(bf16)
        gate_ref[u] = jnp.concatenate(
            [jnp.concatenate(gates[:2], axis=1), jnp.concatenate(gates[2:], axis=1)], axis=0
        ).astype(bf16)
        return before, second

    zero = [jnp.zeros((24, LANES), f32)] * (TAPS - 1)
    lax.fori_loop(0, 32, place, (zero, jnp.zeros((8, 256), f32)))
    fetch.wait()

    for part in range(4):
        begin = 128 * part
        count = 512 - begin

        def multiply(f, carry, begin=begin, count=count, part=part):
            at = pl.multiple_of(128 + begin - 16 * f, 16)
            m = 4 * f
            right = jnp.concatenate(
                [
                    jnp.concatenate([blocks_ref[m + k] for k in (1, 0, 3, 2)], axis=0),
                    jnp.concatenate([blocks_ref[m + k] for k in (2, 1, 4, 3)], axis=0),
                ],
                axis=1,
            )
            product = jnp.dot(
                rows_ref[pl.ds(at, count), :], right, preferred_element_type=f32
            )
            if part == 0:

                @pl.when(f == 0)
                def _():
                    acc_ref[...] = product

                @pl.when(f > 0)
                def _():
                    acc_ref[...] += product

            else:
                acc_ref[begin:, :] += product
            return carry

        lax.fori_loop(8 * part, 8 * part + 8, multiply, 0)

    skip = jnp.broadcast_to(skip_ref[...], (16, 256))

    def finish(u, carry):
        at = pl.ds(pl.multiple_of(16 * u, 16), 16)
        here = pl.ds(pl.multiple_of(128 + 16 * u, 16), 16)
        total = acc_ref[at, :] + skip * rows_ref[here, 0:256].astype(f32)
        out_ref[u] = (gate_ref[u].astype(f32) * total).astype(bf16)
        return carry

    lax.fori_loop(0, 32, finish, 0, unroll=4)


def conv_rows(table, recv, reach, taps, skip, blocks):
    whole = pl.BlockSpec(memory_space=pltpu.VMEM)
    return pl.pallas_call(
        conv_kernel,
        in_specs=[pl.BlockSpec(memory_space=pltpu.SMEM)] + [whole] * 4
        + [pl.BlockSpec(memory_space=pltpu.HBM)],
        out_specs=whole,
        out_shape=jax.ShapeDtypeStruct((32, 16, 256), bf16),
        scratch_shapes=[
            pltpu.VMEM((640, 512), bf16),
            pltpu.VMEM((512, 256), f32),
            pltpu.VMEM((32, 16, 256), bf16),
            pltpu.VMEM((129, LANES, LANES), bf16),
            pltpu.SemaphoreType.DMA,
        ],
        compiler_params=vmem(20),
        name="conv_rows",
    )(table, recv, reach, taps, skip, blocks)


def power_kernel(in_ref, out_ref):
    for half in range(2):
        block = in_ref[:, 8 * half : 8 * half + 8, :].astype(f32).reshape(256, 256)
        out_ref[half : half + 1, :] = jnp.sum(block * block, axis=0, keepdims=True)


def power_rows(rows):
    return pl.pallas_call(
        power_kernel,
        out_shape=jax.ShapeDtypeStruct((2, 256), f32),
        compiler_params=vmem(4),
        name="power_rows",
    )(rows)


def turn_kernel(in_ref, out_ref):
    for half in range(2):
        block = in_ref[:, 8 * half : 8 * half + 8, :].astype(f32).reshape(256, 256)
        out_ref[256 * half : 256 * half + 256, :] = jnp.transpose(block).astype(bf16)


def turn_rows(rows):
    return pl.pallas_call(
        turn_kernel,
        out_shape=jax.ShapeDtypeStruct((512, 256), bf16),
        compiler_params=vmem(4),
        name="turn_rows",
    )(rows)


def exchange(block, axis):
    return lax.all_to_all(block, axis, split_axis=0, concat_axis=0, tiled=True)


def local(
    loaded, dest_tiles, tile_counts, segments, short_filters, long_filters, skip_gain, norm_gain
):
    position = lax.axis_index("seq")
    recv = exchange(pack(loaded), "seq")

    slots = jnp.concatenate(
        [dest_tiles // 16, dest_tiles % 16, tile_counts, jnp.zeros((447,), jnp.int32)]
    )
    notes = jnp.concatenate(
        [segments[None], slots[None], jnp.zeros((6, 512), jnp.int32)], axis=0
    ).astype(bf16)
    known = lax.all_gather(jnp.concatenate([long_filters, notes], axis=0), "seq")
    lags = lax.dynamic_slice_in_dim(known, position // 2, 1, 1)
    lags = lags.reshape(LANES, 1, LANES).astype(f32)
    seg = known[:, 16].astype(jnp.int32).reshape(-1)
    slots = known[:, 17].astype(jnp.int32)
    placed = slots[:, 0:32] * 16 + slots[:, 32:64]
    used = jnp.arange(32, dtype=jnp.int32)[None, :] < slots[:, 64:65]
    placed = jnp.where(used, placed, -1).reshape(-1)
    tiles = jnp.arange(512, dtype=jnp.int32)
    slot_ids = jnp.arange(1024, dtype=jnp.int32)
    table = jnp.sum(
        jnp.where(placed[None, :] == tiles[:, None], slot_ids[None, :], 0), axis=1
    ).astype(jnp.int32)
    reach = jnp.zeros(seg.shape, jnp.int32)
    for j in range(1, TAPS):
        reach = reach + jnp.concatenate(
            [jnp.zeros((j,), jnp.int32), (seg[j:] == seg[:-j]).astype(jnp.int32)]
        )
    reach = reach.reshape(LANES, LANES)

    taps = lax.dynamic_slice_in_dim(short_filters, position * 8, 8, 2)
    taps = jnp.broadcast_to(taps[..., None], (3, TAPS, 8, LANES))
    taps = jnp.transpose(taps, (1, 0, 2, 3)).reshape(TAPS, 24, LANES)
    skip = lax.dynamic_slice_in_dim(skip_gain, position * 8, 8, 0)
    skip = jnp.tile(skip, 2)[:, None]

    gated = conv_rows(table, recv, reach, taps, skip, pltpu.with_memory_space_constraint(toeplitz_blocks(lags), pltpu.HBM))
    mine = exchange(gated, "seq")
    power = power_rows(mine).reshape(-1)
    every = exchange(jnp.broadcast_to(power[None], (16, 512)), "chan")
    scale = lax.rsqrt(jnp.sum(every, axis=0) / 4096.0 + 1e-06)
    rows = turn_rows(mine)
    return (rows.astype(f32) * scale[:, None] * norm_gain[None, :]).astype(bf16)


def solution(mesh):
    return jax.shard_map(
        local,
        mesh=mesh,
        in_specs=(
            P(None, "seq", "chan"),
            P("seq"),
            P("seq"),
            P("seq"),
            P(None, None, "chan"),
            P("chan", "seq"),
            P("chan"),
            P("chan"),
        ),
        out_specs=P("seq", "chan"),
        check_vma=False,
    )
```

time: 183 us -> 189 us (1.033)
  blocking collectives: 25.4 us -> 128 us
  waiting for transfers between devices: 77.3 us -> 6.34 us
  Pallas kernels: 35.5 us -> 22.8 us
  local copies, waits for them, and re-layouts: 11.9 us -> 4.77 us
  starting transfers between devices: 27.7 us -> 23.6 us
    all_gather x0 -> x1, blocking collectives: none -> 95.8 us  [local(): lax.all_gather(jnp.concatenate([long_filters, notes], axis=0), 'seq')]
    all_to_all x3 -> x2, waiting for transfers between devices: 77.3 us -> 6.34 us  [exchange(): return lax.all_to_all(block, axis, split_axis=0, concat_axis=0, tiled=True)]
    pallas_call x4 -> x2, Pallas kernels: 19.3 us -> 6.19 us  [the longest x1 3.73 us: pack(): pl.pallas_call(pack_kernel, grid=(8,), in_specs=[pl.BlockSpec((3, LANES,...]
    all_to_all x1, blocking collectives: 25.4 us -> 32.4 us  [exchange(): return lax.all_to_all(block, axis, split_axis=0, concat_axis=0, tiled=True)]
    unnamed x17, local copies, waits for them, and re-layouts: 9.03 us -> 3.39 us
    all_to_all x3 -> x2, starting transfers between devices: 27.7 us -> 23.6 us  [exchange(): return lax.all_to_all(block, axis, split_axis=0, concat_axis=0, tiled=True)]
  transfers between devices with their start and end apart: 3 -> 2, of which waited for: 3 -> 1; matrix products, arithmetic and copies ran while one was open for 1% -> 1% of each run, Pallas kernels for 10% -> 1%
where the time goes in v2:
time: 189 us
  blocking collectives  128 us (68%)
  starting transfers between devices  23.6 us (12%)
  Pallas kernels  22.8 us (12%)
  waiting for transfers between devices  6.34 us (3%)
  local copies, waits for them, and re-layouts  4.77 us (3%)
  other arithmetic  2.32 us (1%)
    all_gather x1, blocking collectives, local(): lax.all_gather(jnp.concatenate([long_filters, notes], axis=0), 'seq')  95.8 us
    all_to_all x1, blocking collectives, exchange(): return lax.all_to_all(block, axis, split_axis=0, concat_axis=0, tiled=True)  32.4 us
    all_to_all x2, starting transfers between devices, exchange(): return lax.all_to_all(block, axis, split_axis=0, concat_axis=0, tiled=True)  23.6 us
    pallas_call x1, Pallas kernels, conv_rows(): pl.pallas_call(conv_kernel, in_specs=[pl.BlockSpec(memory_space=pltpu.SME...  16.4 us
    all_to_all x2, waiting for transfers between devices, exchange(): return lax.all_to_all(block, axis, split_axis=0, concat_axis=0, tiled=True)  6.34 us
  transfers between devices with their start and end apart: 2, of which 1 were waited for; matrix products, arithmetic and copies ran while one was open for 1% of the time, Pallas kernels for 1%

profile of v2, /device:TPU:1, one launch (start us, length us, event | category | flops | bytes accessed | tf_op | source)
XLA Modules:
  0.0 188.9 jit_solution(2772647079831236885)
XLA Ops:
  0.0 0.0 copy-start
  0.0 0.0 copy-start.2
  0.0 1.4 copy-done.2
  1.4 3.7 %pack.1 = bf16[32,8,24,128]{3,2,1,0:T(8,128)(2,1)} custom-call(bf16[3,1024,256]{2,1,0:T(8,128)(2,1)S(1)} %copy-done.2), custom_call_target="tpu_custom_call" | custom-call | tf_op jit(solution)/shard_map/pack/pallas_call | solution.py:30
  5.1 0.0 copy-start.4
  5.2 0.0 copy-start.7
  5.2 0.0 copy-start.6
  5.2 0.0 copy-start.3
  5.2 16.9 %all-to-all-start = ((bf16[32,8,24,128]{3,2,1,0:T(8,128)(2,1)}), bf16[32,8,24,128]{3,2,1,0:T(8,128)(2,1)S(1)}, u32[]{:S(2)}, u32[]{:S(2)}) async-start(bf16[32,8,24,128]{3,2,1,0:T(8,128)(2,1)} %pack.1), calls=%async_computation | async-start | bytes 3145728 | tf_op jit(solution)/shard_map/all_to_all | solution.py:216
  22.7 0.0 copy-done.4
  22.8 0.0 copy-done.7
  22.8 0.1 pad_maximum_fusion
  22.9 0.0 copy-done.6
  22.9 0.1 dynamic_slice.10
  23.0 0.1 broadcast_in_dim_tile.4.skip_ref
  23.1 0.0 copy-done
  23.1 0.1 constant_dynamic-slice_fusion.1
  23.2 0.1 pad.15.clone
  23.2 0.0 copy-done.3
  23.2 0.1 maximum_maximum_fusion
  23.3 95.8 %all-gather = bf16[768,512]{1,0:T(8,128)(2,1)S(1)} all-gather(bf16[24,512]{1,0:T(8,128)(2,1)S(1)} %maximum_maximum_fusion), channel_id=2, replica_groups=mesh['seq'=32,'chan'=16] {'seq'}, dimensions={0}, use_global_device_ids=true | all-gather | bytes 811008 | tf_op jit(solution)/shard_map/all_gather | solution.py:231
  119.1 0.2 constant_dynamic-slice_fusion
  119.3 0.1 reshape.48.lags_ref
  119.4 0.2 slice_reduce_fusion
  119.6 0.1 fusion.1
  119.6 0.1 eq.35
  119.7 2.5 %toeplitz_blocks.1.lags_ref = bf16[129,128,128]{2,1,0:T(8,128)(2,1)S(1)} custom-call(f32[128,1,128]{2,1,0:T(1,128)S(1)} %reshape.48.lags_ref), custom_call_target="tpu_custom_call" | custom-call | tf_op jit(solution)/shard_map/toeplitz_blocks/pallas_call | solution.py:60
  122.2 0.0 copy-start.1
  122.2 1.9 %copy-done.1 = bf16[129,128,128]{2,1,0:T(8,128)(2,1)} copy-done((bf16[129,128,128]{2,1,0:T(8,128)(2,1)}, bf16[129,128,128]{2,1,0:T(8,128)(2,1)S(1)}, u32[]{:S(2)}) %copy-start.1) | copy-done | bytes 4227096
  124.1 0.1 slice_compare_fusion.3
  124.2 0.1 slice_compare_fusion
  124.3 0.1 slice_compare_fusion.4
  124.4 0.1 slice_compare_fusion.2
  124.5 0.1 slice_compare_fusion.5
  124.6 0.1 slice_compare_fusion.1
  124.7 0.2 add_bitcast_fusion.reach_ref
  124.9 0.3 select_reduce_fusion.table_ref
  125.2 0.1 broadcast_bitcast_fusion.taps_ref
  125.3 0.0 copy-start.5
  125.3 0.0 all-to-all-done.recv_ref
  125.3 16.4 %conv_rows.1 = bf16[32,16,256]{2,1,0:T(8,128)(2,1)S(1)} custom-call(s32[512]{0:T(512)S(1)} %select_reduce_fusion.table_ref, bf16[32,8,24,128]{3,2,1,0:T(8,128)(2,1)S(1)} %all-to-all-done.recv_ref, s32[128,128]{1,0:T(8,128)S(1)} %add_bitcast_fusion.reach_ref, f32[7,24,128]{2,1,0:T(8,128)S(1)} %broadcast_bitcast_fusion.taps_ref, ...), custom_call_target="tpu_custom_call" | custom-call | tf_op jit(solution)/shard_map/conv_rows/pallas_call | solution.py:167
  141.7 32.4 %all_to_all.16.in_ref = bf16[32,16,256]{2,1,0:T(8,128)(2,1)S(1)} all-to-all(bf16[32,16,256]{2,1,0:T(8,128)(2,1)S(1)} %conv_rows.1), channel_id=1, replica_groups=mesh['seq'=32,'chan'=16] {'seq'}, dimensions={0} | all-to-all | bytes 524288 | tf_op jit(solution)/shard_map/all_to_all | solution.py:216
  174.2 0.6 broadcast_in_dim.57
  174.8 6.8 %all-to-all-start.2 = ((f32[16,1,512]{2,1,0:T(1,128)}), f32[16,1,512]{2,1,0:T(1,128)S(1)}, u32[]{:S(2)}, u32[]{:S(2)}) async-start(f32[16,1,512]{2,1,0:T(1,128)} %broadcast_in_dim.57), calls=%async_computation.2 | async-start | bytes 65536 | tf_op jit(solution)/shard_map/all_to_all | solution.py:216
  181.6 0.1 turn_rows.1
  181.7 6.3 %all-to-all-done.2 = f32[16,1,512]{2,1,0:T(1,128)S(1)} async-done(((f32[16,1,512]{2,1,0:T(1,128)}), f32[16,1,512]{2,1,0:T(1,128)S(1)}, u32[]{:S(2)}, u32[]{:S(2)}) %all-to-all-start.2) | async-done | bytes 32800 | tf_op jit(solution)/shard_map/all_to_all | solution.py:216
  188.1 0.0 copy-done.5
  188.1 0.8 multiply_convert_fusion
  (14 shorter events, 0.2 us)
Async XLA Ops:
  0.0 23.1 %copy-start = (f32[3,7,256]{2,1,0:T(8,128)S(1)}, f32[3,7,256]{2,1,0:T(8,128)}, u32[]{:S(2)}) copy-start(f32[3,7,256]{2,1,0:T(8,128)} %param.12) | copy-start | bytes 64516
  0.0 1.4 copy-start.2
  5.1 17.6 %copy-start.4 = (s32[512]{0:T(512)S(1)}, s32[512]{0:T(512)}, u32[]{:S(2)}) copy-start(s32[512]{0:T(512)} %param.11) | copy-start | bytes 6148
  5.2 17.6 %copy-start.7 = (s32[32]{0:T(128)S(1)}, s32[32]{0:T(128)}, u32[]{:S(2)}) copy-start(s32[32]{0:T(128)} %param.9) | copy-start | bytes 388
  5.2 17.7 %copy-start.6 = (f32[256]{0:T(256)S(1)}, f32[256]{0:T(256)}, u32[]{:S(2)}) copy-start(f32[256]{0:T(256)} %param.14) | copy-start | bytes 3076
  5.2 18.1 %copy-start.3 = (bf16[16,512]{1,0:T(8,128)(2,1)S(1)}, bf16[16,512]{1,0:T(8,128)(2,1)}, u32[]{:S(2)}) copy-start(bf16[16,512]{1,0:T(8,128)(2,1)} %param.13) | copy-start | bytes 49156
  5.2 120.1 %all-to-all-start = ((bf16[32,8,24,128]{3,2,1,0:T(8,128)(2,1)}), bf16[32,8,24,128]{3,2,1,0:T(8,128)(2,1)S(1)}, u32[]{:S(2)}, u32[]{:S(2)}) async-start(bf16[32,8,24,128]{3,2,1,0:T(8,128)(2,1)} %pack.1), calls=%async_computation | async-start | bytes 3145728 | tf_op jit(solution)/shard_map/all_to_all | solution.py:216
  122.2 2.0 %copy-start.1 = (bf16[129,128,128]{2,1,0:T(8,128)(2,1)}, bf16[129,128,128]{2,1,0:T(8,128)(2,1)S(1)}, u32[]{:S(2)}) copy-start(bf16[129,128,128]{2,1,0:T(8,128)(2,1)S(1)} %toeplitz_blocks.1.lags_ref) | copy-start | bytes 12681220
  125.3 62.8 %copy-start.5 = (f32[256]{0:T(256)S(1)}, f32[256]{0:T(256)}, u32[]{:S(2)}) copy-start(f32[256]{0:T(256)} %param.15) | copy-start | bytes 3076
  174.8 13.2 %all-to-all-start.2 = ((f32[16,1,512]{2,1,0:T(1,128)}), f32[16,1,512]{2,1,0:T(1,128)S(1)}, u32[]{:S(2)}, u32[]{:S(2)}) async-start(f32[16,1,512]{2,1,0:T(1,128)} %broadcast_in_dim.57), calls=%async_computation.2 | async-start | bytes 65536 | tf_op jit(solution)/shard_map/all_to_all | solution.py:216

commit v3 on v2

v3 whole, which is shorter than its diff:
```python
import functools

import jax
import jax.numpy as jnp
from jax import lax
from jax.experimental import pallas as pl
from jax.experimental.pallas import tpu as pltpu
from jax.sharding import PartitionSpec as P

TILE = 32
LANES = 128
TAPS = 7
f32 = jnp.float32
bf16 = jnp.bfloat16


def vmem(mib):
    return pltpu.CompilerParams(vmem_limit_bytes=mib << 20)


def turned(block):
    return jnp.transpose(block.astype(f32)).reshape(32, 8, LANES)


def pack_kernel(
    dest_ref, count_ref, loaded_ref, lags_ref, segments_ref, out_ref,
    rows_ref, turned_ref, notes_ref, in_sems, out_sems,
):
    fetches = []
    for i in range(4):
        fetch = pltpu.make_async_copy(
            loaded_ref.at[:, pl.ds(256 * i, 256), :], rows_ref.at[i], in_sems.at[i]
        )
        fetch.start()
        fetches.append(fetch)

    lane = lax.broadcasted_iota(jnp.int32, (1, LANES), 1)
    line = jnp.zeros((1, LANES), jnp.int32)
    for j in range(32):
        high = jnp.where(j < count_ref[0], dest_ref[j] >> 4, 63)
        line = jnp.where(lane == j, high, line)
        line = jnp.where(lane == 32 + j, dest_ref[j] & 15, line)
    common = jnp.concatenate(
        [segments_ref[...].astype(f32), line.astype(f32), jnp.zeros((7, LANES), f32)], axis=0
    )
    lags = lags_ref[...].astype(f32)
    for r in range(16):
        own = [lags[r : r + 1, LANES * j : LANES * j + LANES] for j in range(4)]
        note = jnp.concatenate(own + [common], axis=0).astype(bf16)
        notes_ref[2 * r] = note
        notes_ref[2 * r + 1] = note
    sends = [
        pltpu.make_async_copy(notes_ref, out_ref.at[:, pl.ds(192, 16), :], out_sems.at[4])
    ]
    sends[0].start()

    for i in range(4):
        fetches[i].wait()
        pieces = [
            turned(rows_ref[i, t, LANES * half : LANES * half + LANES, :])
            for t in range(3)
            for half in range(2)
        ]
        turned_ref[i] = jnp.concatenate(pieces, axis=1).astype(bf16)
        send = pltpu.make_async_copy(
            turned_ref.at[i], out_ref.at[:, pl.ds(48 * i, 48), :], out_sems.at[i]
        )
        send.start()
        sends.append(send)
    for send in sends:
        send.wait()


def pack(dest, count, loaded, lags, segments):
    scalars = pl.BlockSpec(memory_space=pltpu.SMEM)
    whole = pl.BlockSpec(memory_space=pltpu.VMEM)
    far = pl.BlockSpec(memory_space=pltpu.HBM)
    return pl.pallas_call(
        pack_kernel,
        in_specs=[scalars, scalars, far, whole, whole],
        out_specs=far,
        out_shape=jax.ShapeDtypeStruct((32, 208, LANES), bf16),
        scratch_shapes=[
            pltpu.VMEM((4, 3, 256, 256), bf16),
            pltpu.VMEM((4, 32, 48, LANES), bf16),
            pltpu.VMEM((32, 16, LANES), bf16),
            pltpu.SemaphoreType.DMA((4,)),
            pltpu.SemaphoreType.DMA((5,)),
        ],
        compiler_params=vmem(12),
        name="pack",
    )(dest, count, pltpu.with_memory_space_constraint(loaded, pltpu.HBM), lags, segments)


def conv_kernel(
    table_ref, recv_ref, taps_ref, skip_ref, out_ref,
    rows_ref, acc_ref, gate_ref, blocks_ref, slots_ref, placed_ref, lags_ref, seg_ref, reach_ref,
):
    rows_ref[0:128, :] = jnp.zeros((128, 512), bf16)

    def widen(s, carry):
        for pair in range(4):
            for t in range(3):
                both = recv_ref[s, 48 * pair + 16 * t : 48 * pair + 16 * t + 16, :].astype(f32)
                slots_ref[8 * s + 2 * pair, 8 * t : 8 * t + 8, :] = both[:8]
                slots_ref[8 * s + 2 * pair + 1, 8 * t : 8 * t + 8, :] = both[8:]
        return carry

    lax.fori_loop(0, 32, widen, 0, unroll=2)
    for s in range(32):
        both = recv_ref[s, 192:208, :].astype(f32)
        lags_ref[s] = both[:8]
        seg_ref[4 * s : 4 * s + 4, :] = both[4:8]

    row = lax.broadcasted_iota(jnp.int32, (LANES, LANES), 0)
    col = lax.broadcasted_iota(jnp.int32, (LANES, LANES), 1)
    seg = seg_ref[...]
    above = pltpu.roll(seg, 1, 0)
    reach = jnp.zeros((LANES, LANES), f32)
    for j in range(1, TAPS):
        delayed = jnp.where(col >= j, pltpu.roll(seg, j, 1), pltpu.roll(above, j, 1))
        inside = (row > 0) | (col >= j)
        reach = reach + jnp.where((delayed == seg) & inside, 1.0, 0.0)
    reach_ref[...] = reach

    upper = col >= row

    def skewed(f, before):
        for k in range(8):
            line = jnp.broadcast_to(lags_ref[2 * f + k // 4, k % 4 : k % 4 + 1, :], (LANES, LANES))
            skew = pltpu.roll(line, 0, 1, stride=1, stride_axis=0)
            blocks_ref[8 * f + k + 1] = jnp.where(upper, skew, before).astype(bf16)
            before = skew
        return before

    blocks_ref[0] = jnp.zeros((LANES, LANES), bf16)
    lax.fori_loop(0, 16, skewed, jnp.zeros((LANES, LANES), f32))

    lane = lax.broadcasted_iota(jnp.int32, (24, LANES), 1)
    group = lane // TILE

    def gather(u, carry):
        for k in range(16):
            column = 16 * u + k
            out = None
            for b in range(4):
                src = table_ref[column * 4 + b]
                tile = pltpu.roll(slots_ref[src >> 2], ((b - src) & 3) * TILE, 1)
                out = tile if out is None else jnp.where(group == b, tile, out)
            placed_ref[column] = out
        return carry

    lax.fori_loop(0, 8, gather, 0)

    def short(u, carry):
        before, last = carry
        mixed = []
        gates = []
        for k in range(4):
            column = 4 * u + k
            block = placed_ref[column]
            limit = jnp.broadcast_to(reach_ref[pl.ds(column, 1), :], (24, LANES))
            rolled = [pltpu.roll(block, j, 1) for j in range(1, TAPS)]
            total = block * taps_ref[0]
            for j in range(1, TAPS):
                delayed = jnp.where(lane >= j, rolled[j - 1], before[j - 1])
                total = total + jnp.where(limit >= j, delayed, 0.0) * taps_ref[j]
            before = rolled
            gates.append(total[:8])
            mixed.append(total[8:16] * total[16:])
        first = jnp.concatenate(mixed[:2], axis=1)
        second = jnp.concatenate(mixed[2:], axis=1)
        at = pl.ds(pl.multiple_of(128 + 16 * u, 16), 16)
        rows_ref[at, 0:256] = jnp.concatenate([first, second], axis=0).astype(bf16)
        rows_ref[at, 256:512] = jnp.concatenate([last, first], axis=0).astype(bf16)
        gate_ref[u] = jnp.concatenate(
            [jnp.concatenate(gates[:2], axis=1), jnp.concatenate(gates[2:], axis=1)], axis=0
        ).astype(bf16)
        return before, second

    zero = [jnp.zeros((24, LANES), f32)] * (TAPS - 1)
    lax.fori_loop(0, 32, short, (zero, jnp.zeros((8, 256), f32)), unroll=2)

    for part in range(4):
        begin = 128 * part
        for f in range(8 * part, 8 * part + 8, 2):
            left, right = [], []
            for g in (f, f + 1):
                at = 128 + begin - 16 * g
                left.append(rows_ref[at : at + 512 - begin, :])
                right.append(
                    jnp.concatenate(
                        [
                            jnp.concatenate([blocks_ref[4 * g + k] for k in (1, 0, 3, 2)], axis=0),
                            jnp.concatenate([blocks_ref[4 * g + k] for k in (2, 1, 4, 3)], axis=0),
                        ],
                        axis=1,
                    )
                )
            product = jnp.dot(
                jnp.concatenate(left, axis=1),
                jnp.concatenate(right, axis=0),
                preferred_element_type=f32,
            )
            if f == 0:
                acc_ref[...] = product
            else:
                acc_ref[begin:, :] += product

    skip = jnp.broadcast_to(skip_ref[...], (16, 256))

    def finish(u, carry):
        at = pl.ds(pl.multiple_of(16 * u, 16), 16)
        here = pl.ds(pl.multiple_of(128 + 16 * u, 16), 16)
        total = acc_ref[at, :] + skip * rows_ref[here, 0:256].astype(f32)
        out_ref[u] = (gate_ref[u].astype(f32) * total).astype(bf16)
        return carry

    lax.fori_loop(0, 32, finish, 0, unroll=4)


def conv_rows(table, recv, taps, skip):
    whole = pl.BlockSpec(memory_space=pltpu.VMEM)
    return pl.pallas_call(
        conv_kernel,
        in_specs=[pl.BlockSpec(memory_space=pltpu.SMEM)] + [whole] * 3,
        out_specs=whole,
        out_shape=jax.ShapeDtypeStruct((32, 16, 256), bf16),
        scratch_shapes=[
            pltpu.VMEM((640, 512), bf16),
            pltpu.VMEM((512, 256), f32),
            pltpu.VMEM((32, 16, 256), bf16),
            pltpu.VMEM((129, LANES, LANES), bf16),
            pltpu.VMEM((256, 24, LANES), f32),
            pltpu.VMEM((LANES, 24, LANES), f32),
            pltpu.VMEM((32, 8, LANES), f32),
            pltpu.VMEM((LANES, LANES), f32),
            pltpu.VMEM((LANES, LANES), f32),
        ],
        compiler_params=vmem(24),
        name="conv_rows",
    )(table, recv, taps, skip)


def power_kernel(in_ref, out_ref):
    for half in range(2):
        block = in_ref[:, 8 * half : 8 * half + 8, :].astype(f32).reshape(256, 256)
        out_ref[half : half + 1, :] = jnp.sum(block * block, axis=0, keepdims=True)


def power_rows(rows):
    return pl.pallas_call(
        power_kernel,
        out_shape=jax.ShapeDtypeStruct((2, 256), f32),
        compiler_params=vmem(4),
        name="power_rows",
    )(rows)


def turn_kernel(in_ref, out_ref):
    for half in range(2):
        block = in_ref[:, 8 * half : 8 * half + 8, :].astype(f32).reshape(256, 256)
        out_ref[256 * half : 256 * half + 256, :] = jnp.transpose(block).astype(bf16)


def turn_rows(rows):
    return pl.pallas_call(
        turn_kernel,
        out_shape=jax.ShapeDtypeStruct((512, 256), bf16),
        compiler_params=vmem(4),
        name="turn_rows",
    )(rows)


def exchange(block, axis):
    return lax.all_to_all(block, axis, split_axis=0, concat_axis=0, tiled=True)


def local(
    loaded, dest_tiles, tile_counts, segments, short_filters, long_filters, skip_gain, norm_gain
):
    position = lax.axis_index("seq")
    recv = exchange(
        pack(dest_tiles, tile_counts, loaded, long_filters, segments.reshape(4, LANES)), "seq"
    )

    slots = recv[:, 200].astype(jnp.int32)
    placed = (slots[:, 0:32] * 16 + slots[:, 32:64]).reshape(-1)
    tiles = jnp.arange(512, dtype=jnp.int32)
    slot_ids = jnp.arange(1024, dtype=jnp.int32)
    table = jnp.sum(
        jnp.where(placed[None, :] == tiles[:, None], slot_ids[None, :], 0), axis=1
    ).astype(jnp.int32)

    taps = lax.dynamic_slice_in_dim(short_filters, position * 8, 8, 2)
    taps = jnp.broadcast_to(taps[..., None], (3, TAPS, 8, LANES))
    taps = jnp.transpose(taps, (1, 0, 2, 3)).reshape(TAPS, 24, LANES)
    skip = lax.dynamic_slice_in_dim(skip_gain, position * 8, 8, 0)
    skip = jnp.tile(skip, 2)[:, None]

    gated = conv_rows(table, recv, taps, skip)
    mine = exchange(gated, "seq")
    power = power_rows(mine).reshape(-1)
    every = exchange(jnp.broadcast_to(power[None], (16, 512)), "chan")
    scale = lax.rsqrt(jnp.sum(every, axis=0) / 4096.0 + 1e-06)
    rows = turn_rows(mine)
    return (rows.astype(f32) * scale[:, None] * norm_gain[None, :]).astype(bf16)


def solution(mesh):
    return jax.shard_map(
        local,
        mesh=mesh,
        in_specs=(
            P(None, "seq", "chan"),
            P("seq"),
            P("seq"),
            P("seq"),
            P(None, None, "chan"),
            P("chan", "seq"),
            P("chan"),
            P("chan"),
        ),
        out_specs=P("seq", "chan"),
        check_vma=False,
    )
```

time: 189 us -> 159 us (0.84)
  blocking collectives: 128 us -> 25.6 us
  waiting for transfers between devices: 6.34 us -> 89.1 us
  Pallas kernels: 22.8 us -> 15.6 us
    all_gather x1 -> x0, blocking collectives: 95.8 us -> none  [local(): lax.all_gather(jnp.concatenate([long_filters, notes], axis=0), 'seq')]
    all_to_all x2, waiting for transfers between devices: 6.34 us -> 89.1 us  [exchange(): return lax.all_to_all(block, axis, split_axis=0, concat_axis=0, tiled=True)]
    all_to_all x1, blocking collectives: 32.4 us -> 25.6 us  [exchange(): return lax.all_to_all(block, axis, split_axis=0, concat_axis=0, tiled=True)]
    pallas_call x1, Pallas kernels: 16.4 us -> 12.3 us  [conv_rows(): pl.pallas_call(conv_kernel, in_specs=[pl.BlockSpec(memory_space=pltpu.SME...]
    pallas_call x2 -> x1, Pallas kernels: 6.19 us -> 3.12 us  [pack(): pl.pallas_call(pack_kernel, in_specs=[scalars, scalars, far, whole, whole...]
  transfers between devices with their start and end apart: 2 -> 2, of which waited for: 1 -> 2; matrix products, arithmetic and copies ran while one was open for 1% -> 0% of each run, Pallas kernels for 1% -> 0%
where the time goes in v3:
time: 159 us
  waiting for transfers between devices  89.1 us (56%)
  blocking collectives  25.6 us (16%)
  starting transfers between devices  23.5 us (15%)
  Pallas kernels  15.6 us (10%)
  local copies, waits for them, and re-layouts  3.11 us (2%)
    all_to_all x2, waiting for transfers between devices, exchange(): return lax.all_to_all(block, axis, split_axis=0, concat_axis=0, tiled=True)  89.1 us
    all_to_all x1, blocking collectives, exchange(): return lax.all_to_all(block, axis, split_axis=0, concat_axis=0, tiled=True)  25.6 us
    all_to_all x2, starting transfers between devices, exchange(): return lax.all_to_all(block, axis, split_axis=0, concat_axis=0, tiled=True)  23.5 us
    pallas_call x1, Pallas kernels, conv_rows(): pl.pallas_call(conv_kernel, in_specs=[pl.BlockSpec(memory_space=pltpu.SME...  12.3 us
  transfers between devices with their start and end apart: 2, of which 2 were waited for; matrix products, arithmetic and copies ran while one was open for 0% of the time, Pallas kernels for 0%

profile of v3, /device:TPU:1, one launch (start us, length us, event | category | flops | bytes accessed | tf_op | source)
XLA Modules:
  0.0 158.9 jit_solution(14734593745128385411)
XLA Ops:
  0.0 0.0 copy-start
  0.7 0.0 copy-start.1
  0.7 0.7 copy-done.1
  1.4 0.0 copy-start.2
  1.4 0.7 copy-done.2
  2.1 0.0 copy-start.3
  2.1 0.7 copy-done.3
  2.7 3.1 %pack.1 = bf16[32,208,128]{2,1,0:T(8,128)(2,1)} custom-call(s32[32]{0:T(128)S(1)} %copy-done.3, s32[1]{0:T(128)S(6)} %copy.18.count_ref, bf16[3,1024,256]{2,1,0:T(8,128)(2,1)} %loaded_ref.1, bf16[16,512]{1,0:T(8,128)(2,1)S(1)} %copy-done.1, s32[4,128]{1,0:T(4,128)S(1)} %bitcast.9), custom_call_target="tpu_custom_call" | custom-call | tf_op jit(solution)/shard_map/pack/pallas_call | solution.py:78
  5.8 0.0 copy-start.5
  5.9 16.8 %all-to-all-start = ((bf16[32,208,128]{2,1,0:T(8,128)(2,1)}), bf16[32,208,128]{2,1,0:T(8,128)(2,1)S(1)}, u32[]{:S(2)}, u32[]{:S(2)}) async-start(bf16[32,208,128]{2,1,0:T(8,128)(2,1)} %pack.1), calls=%async_computation | async-start | bytes 3407872 | tf_op jit(solution)/shard_map/all_to_all | solution.py:276
  22.6 0.0 copy-done
  22.6 0.1 constant_dynamic-slice_fusion
  22.7 0.0 copy-done.5
  22.7 0.1 dynamic_slice.7
  22.8 0.1 broadcast_in_dim_tile.4.skip_ref
  22.9 0.1 broadcast_bitcast_fusion.taps_ref
  23.0 82.8 %all-to-all-done.recv_ref = bf16[32,208,128]{2,1,0:T(8,128)(2,1)S(1)} async-done(((bf16[32,208,128]{2,1,0:T(8,128)(2,1)}), bf16[32,208,128]{2,1,0:T(8,128)(2,1)S(1)}, u32[]{:S(2)}, u32[]{:S(2)}) %all-to-all-start) | async-done | bytes 1703968 | tf_op jit(solution)/shard_map/all_to_all | solution.py:276
  105.8 0.1 slice_add_fusion
  105.8 0.1 eq.15
  105.9 0.3 select_reduce_fusion.table_ref
  106.2 0.0 copy-start.4
  106.2 12.3 %conv_rows.1 = bf16[32,16,256]{2,1,0:T(8,128)(2,1)S(1)} custom-call(s32[512]{0:T(512)S(1)} %select_reduce_fusion.table_ref, bf16[32,208,128]{2,1,0:T(8,128)(2,1)S(1)} %all-to-all-done.recv_ref, f32[7,24,128]{2,1,0:T(8,128)S(1)} %broadcast_bitcast_fusion.taps_ref, f32[16,1]{1,0:T(8,128)S(1)} %broadcast_in_dim_tile.4.skip_ref), custom_call_target="tpu_custom_call" | custom-call | tf_op jit(solution)/shard_map/conv_rows/pallas_call | solution.py:224
  118.5 25.6 %all_to_all.16.in_ref = bf16[32,16,256]{2,1,0:T(8,128)(2,1)S(1)} all-to-all(bf16[32,16,256]{2,1,0:T(8,128)(2,1)S(1)} %conv_rows.1), channel_id=1, replica_groups=mesh['seq'=32,'chan'=16] {'seq'}, dimensions={0} | all-to-all | bytes 524288 | tf_op jit(solution)/shard_map/all_to_all | solution.py:276
  144.1 0.6 broadcast_in_dim.33
  144.8 6.8 %all-to-all-start.2 = ((f32[16,1,512]{2,1,0:T(1,128)}), f32[16,1,512]{2,1,0:T(1,128)S(1)}, u32[]{:S(2)}, u32[]{:S(2)}) async-start(f32[16,1,512]{2,1,0:T(1,128)} %broadcast_in_dim.33), calls=%async_computation.2 | async-start | bytes 65536 | tf_op jit(solution)/shard_map/all_to_all | solution.py:276
  151.5 0.1 turn_rows.1
  151.7 6.3 %all-to-all-done.2 = f32[16,1,512]{2,1,0:T(1,128)S(1)} async-done(((f32[16,1,512]{2,1,0:T(1,128)}), f32[16,1,512]{2,1,0:T(1,128)S(1)}, u32[]{:S(2)}, u32[]{:S(2)}) %all-to-all-start.2) | async-done | bytes 32800 | tf_op jit(solution)/shard_map/all_to_all | solution.py:276
  158.1 0.0 copy-done.4
  158.1 0.8 multiply_convert_fusion
  (7 shorter events, 0.1 us)
Async XLA Ops:
  0.0 22.6 %copy-start = (f32[3,7,256]{2,1,0:T(8,128)S(1)}, f32[3,7,256]{2,1,0:T(8,128)}, u32[]{:S(2)}) copy-start(f32[3,7,256]{2,1,0:T(8,128)} %param.12) | copy-start | bytes 64516
  0.7 0.7 copy-start.1
  1.4 0.7 copy-start.2
  2.1 0.7 copy-start.3
  5.8 16.9 %copy-start.5 = (f32[256]{0:T(256)S(1)}, f32[256]{0:T(256)}, u32[]{:S(2)}) copy-start(f32[256]{0:T(256)} %param.14) | copy-start | bytes 3076
  5.9 99.9 %all-to-all-start = ((bf16[32,208,128]{2,1,0:T(8,128)(2,1)}), bf16[32,208,128]{2,1,0:T(8,128)(2,1)S(1)}, u32[]{:S(2)}, u32[]{:S(2)}) async-start(bf16[32,208,128]{2,1,0:T(8,128)(2,1)} %pack.1), calls=%async_computation | async-start | bytes 3407872 | tf_op jit(solution)/shard_map/all_to_all | solution.py:276
  106.2 51.8 %copy-start.4 = (f32[256]{0:T(256)S(1)}, f32[256]{0:T(256)}, u32[]{:S(2)}) copy-start(f32[256]{0:T(256)} %param.15) | copy-start | bytes 3076
  144.8 13.2 %all-to-all-start.2 = ((f32[16,1,512]{2,1,0:T(1,128)}), f32[16,1,512]{2,1,0:T(1,128)S(1)}, u32[]{:S(2)}, u32[]{:S(2)}) async-start(f32[16,1,512]{2,1,0:T(1,128)} %broadcast_in_dim.33), calls=%async_computation.2 | async-start | bytes 65536 | tf_op jit(solution)/shard_map/all_to_all | solution.py:276

commit v4 on v3

--- a/solution.py
+++ b/solution.py
@@ -23,10 +23,18 @@
 
 
 def pack_kernel(
-    dest_ref, count_ref, loaded_ref, lags_ref, segments_ref, out_ref,
-    rows_ref, turned_ref, notes_ref, in_sems, out_sems,
+    dest_hbm, count_ref, loaded_ref, lags_hbm, segments_hbm, out_ref,
+    rows_ref, turned_ref, notes_ref, dest_ref, lags_ref, segments_ref,
+    in_sems, out_sems, note_sems,
 ):
     fetches = []
+    small = [
+        pltpu.make_async_copy(dest_hbm, dest_ref, note_sems.at[0]),
+        pltpu.make_async_copy(lags_hbm, lags_ref, note_sems.at[1]),
+        pltpu.make_async_copy(segments_hbm, segments_ref, note_sems.at[2]),
+    ]
+    for copy in small:
+        copy.start()
     for i in range(4):
         fetch = pltpu.make_async_copy(
             loaded_ref.at[:, pl.ds(256 * i, 256), :], rows_ref.at[i], in_sems.at[i]
@@ -34,6 +42,8 @@
         fetch.start()
         fetches.append(fetch)
 
+    for copy in small:
+        copy.wait()
     lane = lax.broadcasted_iota(jnp.int32, (1, LANES), 1)
     line = jnp.zeros((1, LANES), jnp.int32)
     for j in range(32):
@@ -73,23 +83,29 @@
 
 def pack(dest, count, loaded, lags, segments):
     scalars = pl.BlockSpec(memory_space=pltpu.SMEM)
-    whole = pl.BlockSpec(memory_space=pltpu.VMEM)
     far = pl.BlockSpec(memory_space=pltpu.HBM)
+    dest, loaded, lags, segments = [
+        pltpu.with_memory_space_constraint(a, pltpu.HBM) for a in (dest, loaded, lags, segments)
+    ]
     return pl.pallas_call(
         pack_kernel,
-        in_specs=[scalars, scalars, far, whole, whole],
+        in_specs=[far, scalars, far, far, far],
         out_specs=far,
         out_shape=jax.ShapeDtypeStruct((32, 208, LANES), bf16),
         scratch_shapes=[
             pltpu.VMEM((4, 3, 256, 256), bf16),
             pltpu.VMEM((4, 32, 48, LANES), bf16),
             pltpu.VMEM((32, 16, LANES), bf16),
+            pltpu.SMEM((32,), jnp.int32),
+            pltpu.VMEM((16, 512), bf16),
+            pltpu.VMEM((4, LANES), jnp.int32),
             pltpu.SemaphoreType.DMA((4,)),
             pltpu.SemaphoreType.DMA((5,)),
+            pltpu.SemaphoreType.DMA((3,)),
         ],
         compiler_params=vmem(12),
         name="pack",
-    )(dest, count, pltpu.with_memory_space_constraint(loaded, pltpu.HBM), lags, segments)
+    )(dest, count, loaded, lags, segments)
 
 
 def conv_kernel(
@@ -122,19 +138,6 @@
         inside = (row > 0) | (col >= j)
         reach = reach + jnp.where((delayed == seg) & inside, 1.0, 0.0)
     reach_ref[...] = reach
-
-    upper = col >= row
-
-    def skewed(f, before):
-        for k in range(8):
-            line = jnp.broadcast_to(lags_ref[2 * f + k // 4, k % 4 : k % 4 + 1, :], (LANES, LANES))
-            skew = pltpu.roll(line, 0, 1, stride=1, stride_axis=0)
-            blocks_ref[8 * f + k + 1] = jnp.where(upper, skew, before).astype(bf16)
-            before = skew
-        return before
-
-    blocks_ref[0] = jnp.zeros((LANES, LANES), bf16)
-    lax.fori_loop(0, 16, skewed, jnp.zeros((LANES, LANES), f32))
 
     lane = lax.broadcasted_iota(jnp.int32, (24, LANES), 1)
     group = lane // TILE
@@ -179,8 +182,12 @@
         return before, second
 
     zero = [jnp.zeros((24, LANES), f32)] * (TAPS - 1)
-    lax.fori_loop(0, 32, short, (zero, jnp.zeros((8, 256), f32)), unroll=2)
-
+    lax.fori_loop(0, 32, short, (zero, jnp.zeros((8, 256), f32)), unroll=4)
+
+
+    upper = col >= row
+    skew = jnp.zeros((LANES, LANES), f32)
+    block = jnp.zeros((LANES, LANES), bf16)
     for part in range(4):
         begin = 128 * part
         for f in range(8 * part, 8 * part + 8, 2):
@@ -188,11 +195,17 @@
             for g in (f, f + 1):
                 at = 128 + begin - 16 * g
                 left.append(rows_ref[at : at + 512 - begin, :])
+                made = [block]
+                for k in range(4):
+                    line = jnp.broadcast_to(lags_ref[g, k : k + 1, :], (LANES, LANES))
+                    before, skew = skew, pltpu.roll(line, 0, 1, stride=1, stride_axis=0)
+                    made.append(jnp.where(upper, skew, before).astype(bf16))
+                block = made[4]
                 right.append(
                     jnp.concatenate(
                         [
-                            jnp.concatenate([blocks_ref[4 * g + k] for k in (1, 0, 3, 2)], axis=0),
-                            jnp.concatenate([blocks_ref[4 * g + k] for k in (2, 1, 4, 3)], axis=0),
+                            jnp.concatenate([made[k] for k in (1, 0, 3, 2)], axis=0),
+                            jnp.concatenate([made[k] for k in (2, 1, 4, 3)], axis=0),
                         ],
                         axis=1,
                     )
@@ -243,33 +256,41 @@
 
 
 def power_kernel(in_ref, out_ref):
+    halves = []
     for half in range(2):
         block = in_ref[:, 8 * half : 8 * half + 8, :].astype(f32).reshape(256, 256)
-        out_ref[half : half + 1, :] = jnp.sum(block * block, axis=0, keepdims=True)
+        halves.append(jnp.sum(block * block, axis=0, keepdims=True))
+    line = jnp.concatenate(halves, axis=1)
+    for i in range(16):
+        out_ref[i] = line
 
 
 def power_rows(rows):
     return pl.pallas_call(
         power_kernel,
-        out_shape=jax.ShapeDtypeStruct((2, 256), f32),
+        out_shape=jax.ShapeDtypeStruct((16, 1, 512), f32),
         compiler_params=vmem(4),
         name="power_rows",
     )(rows)
 
 
-def turn_kernel(in_ref, out_ref):
+def scale_kernel(in_ref, power_ref, gain_ref, out_ref):
+    power = jnp.sum(power_ref[...], axis=0)
+    scale = lax.rsqrt(power / 4096.0 + 1e-06)
+    gain = gain_ref[...]
     for half in range(2):
         block = in_ref[:, 8 * half : 8 * half + 8, :].astype(f32).reshape(256, 256)
+        block = block * scale[:, 256 * half : 256 * half + 256] * gain
         out_ref[256 * half : 256 * half + 256, :] = jnp.transpose(block).astype(bf16)
 
 
-def turn_rows(rows):
+def scale_rows(rows, power, gain):
     return pl.pallas_call(
-        turn_kernel,
+        scale_kernel,
         out_shape=jax.ShapeDtypeStruct((512, 256), bf16),
         compiler_params=vmem(4),
-        name="turn_rows",
-    )(rows)
+        name="scale_rows",
+    )(rows, power, gain)
 
 
 def exchange(block, axis):
@@ -300,11 +321,8 @@
 
     gated = conv_rows(table, recv, taps, skip)
     mine = exchange(gated, "seq")
-    power = power_rows(mine).reshape(-1)
-    every = exchange(jnp.broadcast_to(power[None], (16, 512)), "chan")
-    scale = lax.rsqrt(jnp.sum(every, axis=0) / 4096.0 + 1e-06)
-    rows = turn_rows(mine)
-    return (rows.astype(f32) * scale[:, None] * norm_gain[None, :]).astype(bf16)
+    every = exchange(power_rows(mine), "chan")
+    return scale_rows(mine, every, norm_gain[:, None])
 
 
 def solution(mesh):

time: 159 us -> 154 us (0.969)
  local copies, waits for them, and re-layouts: 3.11 us -> 0.55 us
  Pallas kernels: 15.6 us -> 13.6 us
    pallas_call x1, Pallas kernels: 12.3 us -> 9.36 us  [conv_rows(): pl.pallas_call(conv_kernel, in_specs=[pl.BlockSpec(memory_space=pltpu.SME...]
    unnamed x13 -> x6, local copies, waits for them, and re-layouts: 2.07 us -> 0.02 us
where the time goes in v4:
time: 154 us; the launch traced here: 153 us
  waiting for transfers between devices  89.1 us (58%)
  blocking collectives  25.6 us (17%)
  starting transfers between devices  23.5 us (15%)
  Pallas kernels  13.6 us (9%)
    all_to_all x2, waiting for transfers between devices, exchange(): return lax.all_to_all(block, axis, split_axis=0, concat_axis=0, tiled=True)  89.1 us
    all_to_all x1, blocking collectives, exchange(): return lax.all_to_all(block, axis, split_axis=0, concat_axis=0, tiled=True)  25.6 us
    all_to_all x2, starting transfers between devices, exchange(): return lax.all_to_all(block, axis, split_axis=0, concat_axis=0, tiled=True)  23.5 us
    pallas_call x1, Pallas kernels, conv_rows(): pl.pallas_call(conv_kernel, in_specs=[pl.BlockSpec(memory_space=pltpu.SME...  9.36 us
  transfers between devices with their start and end apart: 2, of which 2 were waited for; matrix products, arithmetic and copies ran while one was open for 0% of the time, Pallas kernels for 0%

profile of v4, /device:TPU:1, one launch (start us, length us, event | category | flops | bytes accessed | tf_op | source)
XLA Modules:
  0.0 153.5 jit_solution(9229722542436705955)
XLA Ops:
  0.0 0.0 copy-start
  0.7 2.7 %pack.1 = bf16[32,208,128]{2,1,0:T(8,128)(2,1)} custom-call(s32[32]{0:T(128)} %dest_hbm.1, s32[1]{0:T(128)S(6)} %copy.17.count_ref, bf16[3,1024,256]{2,1,0:T(8,128)(2,1)} %loaded_ref.1, bf16[16,512]{1,0:T(8,128)(2,1)} %lags_hbm.1, s32[4,128]{1,0:T(4,128)} %bitcast.8), custom_call_target="tpu_custom_call" | custom-call | tf_op jit(solution)/shard_map/pack/pallas_call | solution.py:90
  3.3 0.0 copy-start.2
  3.4 16.8 %all-to-all-start = ((bf16[32,208,128]{2,1,0:T(8,128)(2,1)}), bf16[32,208,128]{2,1,0:T(8,128)(2,1)S(1)}, u32[]{:S(2)}, u32[]{:S(2)}) async-start(bf16[32,208,128]{2,1,0:T(8,128)(2,1)} %pack.1), calls=%async_computation | async-start | bytes 3407872 | tf_op jit(solution)/shard_map/all_to_all | solution.py:297
  20.1 0.0 copy-start.1
  20.1 0.0 copy-done
  20.2 0.1 constant_dynamic-slice_fusion
  20.2 0.0 copy-done.2
  20.2 0.1 dynamic_slice.7
  20.3 0.1 broadcast_in_dim_tile.4.skip_ref
  20.4 0.1 broadcast_bitcast_fusion.taps_ref
  20.5 82.7 %all-to-all-done.recv_ref = bf16[32,208,128]{2,1,0:T(8,128)(2,1)S(1)} async-done(((bf16[32,208,128]{2,1,0:T(8,128)(2,1)}), bf16[32,208,128]{2,1,0:T(8,128)(2,1)S(1)}, u32[]{:S(2)}, u32[]{:S(2)}) %all-to-all-start) | async-done | bytes 1703968 | tf_op jit(solution)/shard_map/all_to_all | solution.py:297
  103.3 0.1 slice_add_fusion
  103.3 0.1 eq.15
  103.4 0.3 select_reduce_fusion.table_ref
  103.7 9.4 %conv_rows.1 = bf16[32,16,256]{2,1,0:T(8,128)(2,1)S(1)} custom-call(s32[512]{0:T(512)S(1)} %select_reduce_fusion.table_ref, bf16[32,208,128]{2,1,0:T(8,128)(2,1)S(1)} %all-to-all-done.recv_ref, f32[7,24,128]{2,1,0:T(8,128)S(1)} %broadcast_bitcast_fusion.taps_ref, f32[16,1]{1,0:T(8,128)S(1)} %broadcast_in_dim_tile.4.skip_ref), custom_call_target="tpu_custom_call" | custom-call | tf_op jit(solution)/shard_map/conv_rows/pallas_call | solution.py:237
  113.1 25.6 %all_to_all.15.in_ref = bf16[32,16,256]{2,1,0:T(8,128)(2,1)S(1)} all-to-all(bf16[32,16,256]{2,1,0:T(8,128)(2,1)S(1)} %conv_rows.1), channel_id=1, replica_groups=mesh['seq'=32,'chan'=16] {'seq'}, dimensions={0} | all-to-all | bytes 524288 | tf_op jit(solution)/shard_map/all_to_all | solution.py:297
  138.7 0.7 power_rows.1
  139.3 6.8 %all-to-all-start.2 = ((f32[16,1,512]{2,1,0:T(1,128)}), f32[16,1,512]{2,1,0:T(1,128)S(1)}, u32[]{:S(2)}, u32[]{:S(2)}) async-start(f32[16,1,512]{2,1,0:T(1,128)} %power_rows.1), calls=%async_computation.2 | async-start | bytes 65536 | tf_op jit(solution)/shard_map/all_to_all | solution.py:297
  146.1 0.0 copy-done.1
  146.1 0.1 copy.16.gain_ref
  146.2 6.3 %all-to-all-done.2.power_ref = f32[16,1,512]{2,1,0:T(1,128)S(1)} async-done(((f32[16,1,512]{2,1,0:T(1,128)}), f32[16,1,512]{2,1,0:T(1,128)S(1)}, u32[]{:S(2)}, u32[]{:S(2)}) %all-to-all-start.2) | async-done | bytes 32800 | tf_op jit(solution)/shard_map/all_to_all | solution.py:297
  152.6 0.9 scale_rows.1
  (3 shorter events, 0.0 us)
Async XLA Ops:
  0.0 20.1 %copy-start = (f32[3,7,256]{2,1,0:T(8,128)S(1)}, f32[3,7,256]{2,1,0:T(8,128)}, u32[]{:S(2)}) copy-start(f32[3,7,256]{2,1,0:T(8,128)} %param.12) | copy-start | bytes 64516
  3.3 16.9 %copy-start.2 = (f32[256]{0:T(256)S(1)}, f32[256]{0:T(256)}, u32[]{:S(2)}) copy-start(f32[256]{0:T(256)} %param.14) | copy-start | bytes 3076
  3.4 99.9 %all-to-all-start = ((bf16[32,208,128]{2,1,0:T(8,128)(2,1)}), bf16[32,208,128]{2,1,0:T(8,128)(2,1)S(1)}, u32[]{:S(2)}, u32[]{:S(2)}) async-start(bf16[32,208,128]{2,1,0:T(8,128)(2,1)} %pack.1), calls=%async_computation | async-start | bytes 3407872 | tf_op jit(solution)/shard_map/all_to_all | solution.py:297
  20.1 126.0 %copy-start.1 = (f32[256]{0:T(256)S(1)}, f32[256]{0:T(256)}, u32[]{:S(2)}) copy-start(f32[256]{0:T(256)} %param.15) | copy-start | bytes 3076
  139.3 13.2 %all-to-all-start.2 = ((f32[16,1,512]{2,1,0:T(1,128)}), f32[16,1,512]{2,1,0:T(1,128)S(1)}, u32[]{:S(2)}, u32[]{:S(2)}) async-start(f32[16,1,512]{2,1,0:T(1,128)} %power_rows.1), calls=%async_computation.2 | async-start | bytes 65536 | tf_op jit(solution)/shard_map/all_to_all | solution.py:297

commit v5 on v4

--- a/solution.py
+++ b/solution.py
@@ -50,9 +50,14 @@
         high = jnp.where(j < count_ref[0], dest_ref[j] >> 4, 63)
         line = jnp.where(lane == j, high, line)
         line = jnp.where(lane == 32 + j, dest_ref[j] & 15, line)
-    common = jnp.concatenate(
-        [segments_ref[...].astype(f32), line.astype(f32), jnp.zeros((7, LANES), f32)], axis=0
-    )
+    index = lax.broadcasted_iota(jnp.int32, (LANES, LANES), 0)
+    fewer = jnp.zeros((LANES, LANES), f32)
+    for j in range(4):
+        fewer = fewer + jnp.where(segments_ref[j : j + 1, :] < (index & 63), 1.0, 0.0)
+    below = jnp.sum(fewer, axis=1, keepdims=True).astype(jnp.int32)
+    below = jnp.where(index[:, :1] < 64, below >> 4, below & 15).astype(f32)
+    below = jnp.transpose(jnp.broadcast_to(below, (LANES, LANES)))[:1]
+    common = jnp.concatenate([below, line.astype(f32), jnp.zeros((2, LANES), f32)], axis=0)
     lags = lags_ref[...].astype(f32)
     for r in range(16):
         own = [lags[r : r + 1, LANES * j : LANES * j + LANES] for j in range(4)]
@@ -60,7 +65,7 @@
         notes_ref[2 * r] = note
         notes_ref[2 * r + 1] = note
     sends = [
-        pltpu.make_async_copy(notes_ref, out_ref.at[:, pl.ds(192, 16), :], out_sems.at[4])
+        pltpu.make_async_copy(notes_ref, out_ref.at[:, pl.ds(192, 8), :], out_sems.at[4])
     ]
     sends[0].start()
 
@@ -91,11 +96,11 @@
         pack_kernel,
         in_specs=[far, scalars, far, far, far],
         out_specs=far,
-        out_shape=jax.ShapeDtypeStruct((32, 208, LANES), bf16),
+        out_shape=jax.ShapeDtypeStruct((32, 200, LANES), bf16),
         scratch_shapes=[
             pltpu.VMEM((4, 3, 256, 256), bf16),
             pltpu.VMEM((4, 32, 48, LANES), bf16),
-            pltpu.VMEM((32, 16, LANES), bf16),
+            pltpu.VMEM((32, 8, LANES), bf16),
             pltpu.SMEM((32,), jnp.int32),
             pltpu.VMEM((16, 512), bf16),
             pltpu.VMEM((4, LANES), jnp.int32),
@@ -110,7 +115,7 @@
 
 def conv_kernel(
     table_ref, recv_ref, taps_ref, skip_ref, out_ref,
-    rows_ref, acc_ref, gate_ref, blocks_ref, slots_ref, placed_ref, lags_ref, seg_ref, reach_ref,
+    rows_ref, acc_ref, gate_ref, slots_ref, placed_ref, lags_ref, starts_ref, reach_ref,
 ):
     rows_ref[0:128, :] = jnp.zeros((128, 512), bf16)
 
@@ -123,28 +128,33 @@
         return carry
 
     lax.fori_loop(0, 32, widen, 0, unroll=2)
+    total = jnp.zeros((8, LANES), f32)
     for s in range(32):
-        both = recv_ref[s, 192:208, :].astype(f32)
-        lags_ref[s] = both[:8]
-        seg_ref[4 * s : 4 * s + 4, :] = both[4:8]
-
+        note = recv_ref[s, 192:200, :].astype(f32)
+        lags_ref[s] = note
+        total = total + note
+
+    starts = 16.0 * total[4:5] + pltpu.roll(total[4:5], 64, 1)
+    starts_ref[...] = jnp.transpose(jnp.broadcast_to(starts, (LANES, LANES)))
     row = lax.broadcasted_iota(jnp.int32, (LANES, LANES), 0)
     col = lax.broadcasted_iota(jnp.int32, (LANES, LANES), 1)
-    seg = seg_ref[...]
-    above = pltpu.roll(seg, 1, 0)
-    reach = jnp.zeros((LANES, LANES), f32)
-    for j in range(1, TAPS):
-        delayed = jnp.where(col >= j, pltpu.roll(seg, j, 1), pltpu.roll(above, j, 1))
-        inside = (row > 0) | (col >= j)
-        reach = reach + jnp.where((delayed == seg) & inside, 1.0, 0.0)
-    reach_ref[...] = reach
+    here = (row * LANES + col).astype(f32)
+
+    def latest(v, begin):
+        for k in range(8):
+            start = jnp.broadcast_to(starts_ref[pl.ds(8 * v + k, 1), :], (LANES, LANES))
+            begin = jnp.where(start <= here, start, begin)
+        return begin
+
+    begin = lax.fori_loop(0, 8, latest, jnp.zeros((LANES, LANES), f32))
+    reach_ref[...] = jnp.minimum(here - begin, 6.0)
 
     lane = lax.broadcasted_iota(jnp.int32, (24, LANES), 1)
     group = lane // TILE
 
     def gather(u, carry):
-        for k in range(16):
-            column = 16 * u + k
+        for k in range(32):
+            column = 32 * u + k
             out = None
             for b in range(4):
                 src = table_ref[column * 4 + b]
@@ -153,7 +163,7 @@
             placed_ref[column] = out
         return carry
 
-    lax.fori_loop(0, 8, gather, 0)
+    lax.fori_loop(0, 4, gather, 0)
 
     def short(u, carry):
         before, last = carry
@@ -182,7 +192,7 @@
         return before, second
 
     zero = [jnp.zeros((24, LANES), f32)] * (TAPS - 1)
-    lax.fori_loop(0, 32, short, (zero, jnp.zeros((8, 256), f32)), unroll=4)
+    lax.fori_loop(0, 32, short, (zero, jnp.zeros((8, 256), f32)), unroll=16)
 
 
     upper = col >= row
@@ -243,7 +253,6 @@
             pltpu.VMEM((640, 512), bf16),
             pltpu.VMEM((512, 256), f32),
             pltpu.VMEM((32, 16, 256), bf16),
-            pltpu.VMEM((129, LANES, LANES), bf16),
             pltpu.VMEM((256, 24, LANES), f32),
             pltpu.VMEM((LANES, 24, LANES), f32),
             pltpu.VMEM((32, 8, LANES), f32),
@@ -305,7 +314,7 @@
         pack(dest_tiles, tile_counts, loaded, long_filters, segments.reshape(4, LANES)), "seq"
     )
 
-    slots = recv[:, 200].astype(jnp.int32)
+    slots = recv[:, 197].astype(jnp.int32)
     placed = (slots[:, 0:32] * 16 + slots[:, 32:64]).reshape(-1)
     tiles = jnp.arange(512, dtype=jnp.int32)
     slot_ids = jnp.arange(1024, dtype=jnp.int32)

time: 154 us -> 151 us (0.981)
  waiting for transfers between devices: 89.1 us -> 86.4 us
    all_to_all x2, waiting for transfers between devices: 89.1 us -> 86.4 us  [exchange(): return lax.all_to_all(block, axis, split_axis=0, concat_axis=0, tiled=True)]
where the time goes in v5:
time: 151 us; the launch traced here: 150 us
  waiting for transfers between devices  86.4 us (57%)
  blocking collectives  25.4 us (17%)
  starting transfers between devices  23.5 us (16%)
  Pallas kernels  13.3 us (9%)
    all_to_all x2, waiting for transfers between devices, exchange(): return lax.all_to_all(block, axis, split_axis=0, concat_axis=0, tiled=True)  86.4 us
    all_to_all x1, blocking collectives, exchange(): return lax.all_to_all(block, axis, split_axis=0, concat_axis=0, tiled=True)  25.4 us
    all_to_all x2, starting transfers between devices, exchange(): return lax.all_to_all(block, axis, split_axis=0, concat_axis=0, tiled=True)  23.5 us
    pallas_call x1, Pallas kernels, conv_rows(): pl.pallas_call(conv_kernel, in_specs=[pl.BlockSpec(memory_space=pltpu.SME...  8.94 us
  transfers between devices with their start and end apart: 2, of which 2 were waited for; matrix products, arithmetic and copies ran while one was open for 0% of the time, Pallas kernels for 0%

profile of v5, /device:TPU:1, one launch (start us, length us, event | category | flops | bytes accessed | tf_op | source)
XLA Modules:
  0.0 150.4 jit_solution(15949298554657274445)
XLA Ops:
  0.0 0.0 copy-start
  0.7 2.8 %pack.1 = bf16[32,200,128]{2,1,0:T(8,128)(2,1)} custom-call(s32[32]{0:T(128)} %dest_hbm.1, s32[1]{0:T(128)S(6)} %copy.17.count_ref, bf16[3,1024,256]{2,1,0:T(8,128)(2,1)} %loaded_ref.1, bf16[16,512]{1,0:T(8,128)(2,1)} %lags_hbm.1, s32[4,128]{1,0:T(4,128)} %bitcast.8), custom_call_target="tpu_custom_call" | custom-call | tf_op jit(solution)/shard_map/pack/pallas_call | solution.py:95
  3.5 0.0 copy-start.2
  3.5 16.8 %all-to-all-start = ((bf16[32,200,128]{2,1,0:T(8,128)(2,1)}), bf16[32,200,128]{2,1,0:T(8,128)(2,1)S(1)}, u32[]{:S(2)}, u32[]{:S(2)}) async-start(bf16[32,200,128]{2,1,0:T(8,128)(2,1)} %pack.1), calls=%async_computation | async-start | bytes 3276800 | tf_op jit(solution)/shard_map/all_to_all | solution.py:306
  20.3 0.0 copy-start.1
  20.3 0.0 copy-done
  20.3 0.1 constant_dynamic-slice_fusion
  20.4 0.0 copy-done.2
  20.4 0.1 dynamic_slice.7
  20.5 0.1 broadcast_in_dim_tile.4.skip_ref
  20.5 0.1 broadcast_bitcast_fusion.taps_ref
  20.6 80.1 %all-to-all-done.recv_ref = bf16[32,200,128]{2,1,0:T(8,128)(2,1)S(1)} async-done(((bf16[32,200,128]{2,1,0:T(8,128)(2,1)}), bf16[32,200,128]{2,1,0:T(8,128)(2,1)S(1)}, u32[]{:S(2)}, u32[]{:S(2)}) %all-to-all-start) | async-done | bytes 1638432 | tf_op jit(solution)/shard_map/all_to_all | solution.py:306
  100.8 0.1 slice_add_fusion
  100.9 0.1 eq.15
  100.9 0.3 select_reduce_fusion.table_ref
  101.2 8.9 %conv_rows.1 = bf16[32,16,256]{2,1,0:T(8,128)(2,1)S(1)} custom-call(s32[512]{0:T(512)S(1)} %select_reduce_fusion.table_ref, bf16[32,200,128]{2,1,0:T(8,128)(2,1)S(1)} %all-to-all-done.recv_ref, f32[7,24,128]{2,1,0:T(8,128)S(1)} %broadcast_bitcast_fusion.taps_ref, f32[16,1]{1,0:T(8,128)S(1)} %broadcast_in_dim_tile.4.skip_ref), custom_call_target="tpu_custom_call" | custom-call | tf_op jit(solution)/shard_map/conv_rows/pallas_call | solution.py:247
  110.2 25.4 %all_to_all.15.in_ref = bf16[32,16,256]{2,1,0:T(8,128)(2,1)S(1)} all-to-all(bf16[32,16,256]{2,1,0:T(8,128)(2,1)S(1)} %conv_rows.1), channel_id=1, replica_groups=mesh['seq'=32,'chan'=16] {'seq'}, dimensions={0} | all-to-all | bytes 524288 | tf_op jit(solution)/shard_map/all_to_all | solution.py:306
  135.6 0.7 power_rows.1
  136.2 6.8 %all-to-all-start.2 = ((f32[16,1,512]{2,1,0:T(1,128)}), f32[16,1,512]{2,1,0:T(1,128)S(1)}, u32[]{:S(2)}, u32[]{:S(2)}) async-start(f32[16,1,512]{2,1,0:T(1,128)} %power_rows.1), calls=%async_computation.2 | async-start | bytes 65536 | tf_op jit(solution)/shard_map/all_to_all | solution.py:306
  143.0 0.0 copy-done.1
  143.0 0.1 copy.16.gain_ref
  143.2 6.3 %all-to-all-done.2.power_ref = f32[16,1,512]{2,1,0:T(1,128)S(1)} async-done(((f32[16,1,512]{2,1,0:T(1,128)}), f32[16,1,512]{2,1,0:T(1,128)S(1)}, u32[]{:S(2)}, u32[]{:S(2)}) %all-to-all-start.2) | async-done | bytes 32800 | tf_op jit(solution)/shard_map/all_to_all | solution.py:306
  149.5 0.9 scale_rows.1
  (3 shorter events, 0.0 us)
Async XLA Ops:
  0.0 20.3 %copy-start = (f32[3,7,256]{2,1,0:T(8,128)S(1)}, f32[3,7,256]{2,1,0:T(8,128)}, u32[]{:S(2)}) copy-start(f32[3,7,256]{2,1,0:T(8,128)} %param.12) | copy-start | bytes 64516
  3.5 16.9 %copy-start.2 = (f32[256]{0:T(256)S(1)}, f32[256]{0:T(256)}, u32[]{:S(2)}) copy-start(f32[256]{0:T(256)} %param.14) | copy-start | bytes 3076
  3.5 97.3 %all-to-all-start = ((bf16[32,200,128]{2,1,0:T(8,128)(2,1)}), bf16[32,200,128]{2,1,0:T(8,128)(2,1)S(1)}, u32[]{:S(2)}, u32[]{:S(2)}) async-start(bf16[32,200,128]{2,1,0:T(8,128)(2,1)} %pack.1), calls=%async_computation | async-start | bytes 3276800 | tf_op jit(solution)/shard_map/all_to_all | solution.py:306
  20.3 122.7 %copy-start.1 = (f32[256]{0:T(256)S(1)}, f32[256]{0:T(256)}, u32[]{:S(2)}) copy-start(f32[256]{0:T(256)} %param.15) | copy-start | bytes 3076
  136.2 13.2 %all-to-all-start.2 = ((f32[16,1,512]{2,1,0:T(1,128)}), f32[16,1,512]{2,1,0:T(1,128)S(1)}, u32[]{:S(2)}, u32[]{:S(2)}) async-start(f32[16,1,512]{2,1,0:T(1,128)} %power_rows.1), calls=%async_computation.2 | async-start | bytes 65536 | tf_op jit(solution)/shard_map/all_to_all | solution.py:306

commit v6 on v5

--- a/solution.py
+++ b/solution.py
@@ -42,6 +42,20 @@
         fetch.start()
         fetches.append(fetch)
 
+    sends = []
+    for i in range(4):
+        fetches[i].wait()
+        pieces = [
+            turned(rows_ref[i, t, LANES * half : LANES * half + LANES, :])
+            for t in range(3)
+            for half in range(2)
+        ]
+        turned_ref[i] = jnp.concatenate(pieces, axis=1).astype(bf16)
+        send = pltpu.make_async_copy(
+            turned_ref.at[i], out_ref.at[:, pl.ds(48 * i, 48), :], out_sems.at[i]
+        )
+        send.start()
+        sends.append(send)
     for copy in small:
         copy.wait()
     lane = lax.broadcasted_iota(jnp.int32, (1, LANES), 1)
@@ -64,24 +78,10 @@
         note = jnp.concatenate(own + [common], axis=0).astype(bf16)
         notes_ref[2 * r] = note
         notes_ref[2 * r + 1] = note
-    sends = [
-        pltpu.make_async_copy(notes_ref, out_ref.at[:, pl.ds(192, 8), :], out_sems.at[4])
-    ]
-    sends[0].start()
-
-    for i in range(4):
-        fetches[i].wait()
-        pieces = [
-            turned(rows_ref[i, t, LANES * half : LANES * half + LANES, :])
-            for t in range(3)
-            for half in range(2)
-        ]
-        turned_ref[i] = jnp.concatenate(pieces, axis=1).astype(bf16)
-        send = pltpu.make_async_copy(
-            turned_ref.at[i], out_ref.at[:, pl.ds(48 * i, 48), :], out_sems.at[i]
-        )
-        send.start()
-        sends.append(send)
+    send = pltpu.make_async_copy(notes_ref, out_ref.at[:, pl.ds(192, 8), :], out_sems.at[4])
+    send.start()
+    sends.append(send)
+
     for send in sends:
         send.wait()
 
@@ -152,83 +152,86 @@
     lane = lax.broadcasted_iota(jnp.int32, (24, LANES), 1)
     group = lane // TILE
 
-    def gather(u, carry):
-        for k in range(32):
-            column = 32 * u + k
-            out = None
-            for b in range(4):
-                src = table_ref[column * 4 + b]
-                tile = pltpu.roll(slots_ref[src >> 2], ((b - src) & 3) * TILE, 1)
-                out = tile if out is None else jnp.where(group == b, tile, out)
-            placed_ref[column] = out
-        return carry
-
-    lax.fori_loop(0, 4, gather, 0)
-
-    def short(u, carry):
-        before, last = carry
-        mixed = []
-        gates = []
-        for k in range(4):
-            column = 4 * u + k
-            block = placed_ref[column]
-            limit = jnp.broadcast_to(reach_ref[pl.ds(column, 1), :], (24, LANES))
-            rolled = [pltpu.roll(block, j, 1) for j in range(1, TAPS)]
-            total = block * taps_ref[0]
-            for j in range(1, TAPS):
-                delayed = jnp.where(lane >= j, rolled[j - 1], before[j - 1])
-                total = total + jnp.where(limit >= j, delayed, 0.0) * taps_ref[j]
-            before = rolled
-            gates.append(total[:8])
-            mixed.append(total[8:16] * total[16:])
-        first = jnp.concatenate(mixed[:2], axis=1)
-        second = jnp.concatenate(mixed[2:], axis=1)
-        at = pl.ds(pl.multiple_of(128 + 16 * u, 16), 16)
-        rows_ref[at, 0:256] = jnp.concatenate([first, second], axis=0).astype(bf16)
-        rows_ref[at, 256:512] = jnp.concatenate([last, first], axis=0).astype(bf16)
-        gate_ref[u] = jnp.concatenate(
-            [jnp.concatenate(gates[:2], axis=1), jnp.concatenate(gates[2:], axis=1)], axis=0
-        ).astype(bf16)
-        return before, second
-
-    zero = [jnp.zeros((24, LANES), f32)] * (TAPS - 1)
-    lax.fori_loop(0, 32, short, (zero, jnp.zeros((8, 256), f32)), unroll=16)
-
+    def gather(column):
+        out = None
+        for b in range(4):
+            src = table_ref[column * 4 + b]
+            tile = pltpu.roll(slots_ref[src >> 2], ((b - src) & 3) * TILE, 1)
+            out = tile if out is None else jnp.where(group == b, tile, out)
+        placed_ref[column + 1] = out.astype(bf16)
+
+    ahead = lax.broadcasted_iota(jnp.int32, (256, 768), 0)
+    lag = lax.broadcasted_iota(jnp.int32, (256, 768), 1)
+    shift = (ahead == LANES + (lag & 127) - (lag >> 7) - 1).astype(bf16)
+
+    def short(u, last):
+        now = placed_ref[pl.ds(8 * u + 1, 8)]
+        both = jnp.concatenate(
+            [placed_ref[pl.ds(8 * u, 8)].reshape(192, LANES), now.reshape(192, LANES)], axis=1
+        )
+        delayed = jnp.dot(both, shift, preferred_element_type=f32)
+        for v in range(8 // 4):
+            mixed = []
+            gates = []
+            for k in range(4 * v, 4 * v + 4):
+                limit = jnp.broadcast_to(reach_ref[pl.ds(8 * u + k, 1), :], (24, LANES))
+                total = now[k].astype(f32) * taps_ref[0]
+                for j in range(1, TAPS):
+                    part = delayed[24 * k : 24 * k + 24, LANES * (j - 1) : LANES * j]
+                    total = total + jnp.where(limit >= j, part, 0.0) * taps_ref[j]
+                gates.append(total[:8])
+                mixed.append(total[8:16] * total[16:])
+            first = jnp.concatenate(mixed[:2], axis=1)
+            second = jnp.concatenate(mixed[2:], axis=1)
+            at = pl.ds(128 + 32 * u + 16 * v, 16)
+            rows_ref[at, 0:256] = jnp.concatenate([first, second], axis=0).astype(bf16)
+            rows_ref[at, 256:512] = jnp.concatenate([last, first], axis=0).astype(bf16)
+            gate_ref[2 * u + v] = jnp.concatenate(
+                [jnp.concatenate(gates[:2], axis=1), jnp.concatenate(gates[2:], axis=1)], axis=0
+            ).astype(bf16)
+            last = second
+        return last
+
+    placed_ref[0] = jnp.zeros((24, LANES), bf16)
+    last = jnp.zeros((8, 256), f32)
+    for u in range(16):
+        for k in range(8):
+            gather(8 * u + k)
+        last = short(u, last)
 
     upper = col >= row
     skew = jnp.zeros((LANES, LANES), f32)
     block = jnp.zeros((LANES, LANES), bf16)
-    for part in range(4):
-        begin = 128 * part
-        for f in range(8 * part, 8 * part + 8, 2):
-            left, right = [], []
-            for g in (f, f + 1):
-                at = 128 + begin - 16 * g
-                left.append(rows_ref[at : at + 512 - begin, :])
-                made = [block]
-                for k in range(4):
-                    line = jnp.broadcast_to(lags_ref[g, k : k + 1, :], (LANES, LANES))
-                    before, skew = skew, pltpu.roll(line, 0, 1, stride=1, stride_axis=0)
-                    made.append(jnp.where(upper, skew, before).astype(bf16))
-                block = made[4]
-                right.append(
-                    jnp.concatenate(
-                        [
-                            jnp.concatenate([made[k] for k in (1, 0, 3, 2)], axis=0),
-                            jnp.concatenate([made[k] for k in (2, 1, 4, 3)], axis=0),
-                        ],
-                        axis=1,
-                    )
+    for f in range(0, 32, 2):
+        begin = 16 * f
+        left, right = [], []
+        for g in (f, f + 1):
+            at = 128 + begin - 16 * g
+            left.append(rows_ref[at : at + 512 - begin, :])
+            made = [block]
+            for k in range(4):
+                line = jnp.broadcast_to(lags_ref[g, k : k + 1, :], (LANES, LANES))
+                before, skew = skew, pltpu.roll(line, 0, 1, stride=1, stride_axis=0)
+                made.append(jnp.where(upper, skew, before).astype(bf16))
+            block = made[4]
+            right.append(
+                jnp.concatenate(
+                    [
+                        jnp.concatenate([made[k] for k in (1, 0, 3, 2)], axis=0),
+                        jnp.concatenate([made[k] for k in (2, 1, 4, 3)], axis=0),
+                    ],
+                    axis=1,
                 )
-            product = jnp.dot(
-                jnp.concatenate(left, axis=1),
-                jnp.concatenate(right, axis=0),
-                preferred_element_type=f32,
             )
-            if f == 0:
-                acc_ref[...] = product
-            else:
-                acc_ref[begin:, :] += product
+        product = jnp.dot(
+            jnp.concatenate(left, axis=1),
+            jnp.concatenate(right, axis=0),
+            preferred_element_type=f32,
+        )
+        if f == 0:
+            acc_ref[...] = product
+        else:
+            acc_ref[begin:, :] += product
 
     skip = jnp.broadcast_to(skip_ref[...], (16, 256))
 
@@ -254,7 +257,7 @@
             pltpu.VMEM((512, 256), f32),
             pltpu.VMEM((32, 16, 256), bf16),
             pltpu.VMEM((256, 24, LANES), f32),
-            pltpu.VMEM((LANES, 24, LANES), f32),
+            pltpu.VMEM((LANES + 1, 24, LANES), bf16),
             pltpu.VMEM((32, 8, LANES), f32),
             pltpu.VMEM((LANES, LANES), f32),
             pltpu.VMEM((LANES, LANES), f32),

time: 151 us -> 148 us (0.980)
  Pallas kernels: 13.3 us -> 11 us
    pallas_call x1, Pallas kernels: 8.94 us -> 6.73 us  [conv_rows(): pl.pallas_call(conv_kernel, in_specs=[pl.BlockSpec(memory_space=pltpu.SME...]
where the time goes in v6:
time: 148 us
  waiting for transfers between devices  86.4 us (58%)
  blocking collectives  25.4 us (17%)
  starting transfers between devices  23.5 us (16%)
  Pallas kernels  11 us (7%)
    all_to_all x2, waiting for transfers between devices, exchange(): return lax.all_to_all(block, axis, split_axis=0, concat_axis=0, tiled=True)  86.4 us
    all_to_all x1, blocking collectives, exchange(): return lax.all_to_all(block, axis, split_axis=0, concat_axis=0, tiled=True)  25.4 us
    all_to_all x2, starting transfers between devices, exchange(): return lax.all_to_all(block, axis, split_axis=0, concat_axis=0, tiled=True)  23.5 us
    pallas_call x1, Pallas kernels, conv_rows(): pl.pallas_call(conv_kernel, in_specs=[pl.BlockSpec(memory_space=pltpu.SME...  6.73 us
  transfers between devices with their start and end apart: 2, of which 2 were waited for; matrix products, arithmetic and copies ran while one was open for 0% of the time, Pallas kernels for 0%

profile of v6, /device:TPU:1, one launch (start us, length us, event | category | flops | bytes accessed | tf_op | source)
XLA Modules:
  0.0 148.0 jit_solution(16601463171147330036)
XLA Ops:
  0.0 0.0 copy-start
  0.7 2.6 %pack.1 = bf16[32,200,128]{2,1,0:T(8,128)(2,1)} custom-call(s32[32]{0:T(128)} %dest_hbm.1, s32[1]{0:T(128)S(6)} %copy.17.count_ref, bf16[3,1024,256]{2,1,0:T(8,128)(2,1)} %loaded_ref.1, bf16[16,512]{1,0:T(8,128)(2,1)} %lags_hbm.1, s32[4,128]{1,0:T(4,128)} %bitcast.8), custom_call_target="tpu_custom_call" | custom-call | tf_op jit(solution)/shard_map/pack/pallas_call | solution.py:95
  3.3 0.0 copy-start.2
  3.3 16.8 %all-to-all-start = ((bf16[32,200,128]{2,1,0:T(8,128)(2,1)}), bf16[32,200,128]{2,1,0:T(8,128)(2,1)S(1)}, u32[]{:S(2)}, u32[]{:S(2)}) async-start(bf16[32,200,128]{2,1,0:T(8,128)(2,1)} %pack.1), calls=%async_computation | async-start | bytes 3276800 | tf_op jit(solution)/shard_map/all_to_all | solution.py:309
  20.1 0.0 copy-start.1
  20.1 0.0 copy-done
  20.1 0.1 constant_dynamic-slice_fusion
  20.2 0.0 copy-done.2
  20.2 0.1 dynamic_slice.7
  20.3 0.1 broadcast_in_dim_tile.4.skip_ref
  20.4 0.1 broadcast_bitcast_fusion.taps_ref
  20.5 80.1 %all-to-all-done.recv_ref = bf16[32,200,128]{2,1,0:T(8,128)(2,1)S(1)} async-done(((bf16[32,200,128]{2,1,0:T(8,128)(2,1)}), bf16[32,200,128]{2,1,0:T(8,128)(2,1)S(1)}, u32[]{:S(2)}, u32[]{:S(2)}) %all-to-all-start) | async-done | bytes 1638432 | tf_op jit(solution)/shard_map/all_to_all | solution.py:309
  100.6 0.1 slice_add_fusion
  100.7 0.1 eq.15
  100.8 0.3 select_reduce_fusion.table_ref
  101.1 6.7 %conv_rows.1 = bf16[32,16,256]{2,1,0:T(8,128)(2,1)S(1)} custom-call(s32[512]{0:T(512)S(1)} %select_reduce_fusion.table_ref, bf16[32,200,128]{2,1,0:T(8,128)(2,1)S(1)} %all-to-all-done.recv_ref, f32[7,24,128]{2,1,0:T(8,128)S(1)} %broadcast_bitcast_fusion.taps_ref, f32[16,1]{1,0:T(8,128)S(1)} %broadcast_in_dim_tile.4.skip_ref), custom_call_target="tpu_custom_call" | custom-call | tf_op jit(solution)/shard_map/conv_rows/pallas_call | solution.py:250
  107.8 25.4 %all_to_all.15.in_ref = bf16[32,16,256]{2,1,0:T(8,128)(2,1)S(1)} all-to-all(bf16[32,16,256]{2,1,0:T(8,128)(2,1)S(1)} %conv_rows.1), channel_id=1, replica_groups=mesh['seq'=32,'chan'=16] {'seq'}, dimensions={0} | all-to-all | bytes 524288 | tf_op jit(solution)/shard_map/all_to_all | solution.py:309
  133.2 0.7 power_rows.1
  133.9 6.8 %all-to-all-start.2 = ((f32[16,1,512]{2,1,0:T(1,128)}), f32[16,1,512]{2,1,0:T(1,128)S(1)}, u32[]{:S(2)}, u32[]{:S(2)}) async-start(f32[16,1,512]{2,1,0:T(1,128)} %power_rows.1), calls=%async_computation.2 | async-start | bytes 65536 | tf_op jit(solution)/shard_map/all_to_all | solution.py:309
  140.6 0.0 copy-done.1
  140.6 0.1 copy.16.gain_ref
  140.8 6.3 %all-to-all-done.2.power_ref = f32[16,1,512]{2,1,0:T(1,128)S(1)} async-done(((f32[16,1,512]{2,1,0:T(1,128)}), f32[16,1,512]{2,1,0:T(1,128)S(1)}, u32[]{:S(2)}, u32[]{:S(2)}) %all-to-all-start.2) | async-done | bytes 32800 | tf_op jit(solution)/shard_map/all_to_all | solution.py:309
  147.1 0.9 scale_rows.1
  (3 shorter events, 0.0 us)
Async XLA Ops:
  0.0 20.1 %copy-start = (f32[3,7,256]{2,1,0:T(8,128)S(1)}, f32[3,7,256]{2,1,0:T(8,128)}, u32[]{:S(2)}) copy-start(f32[3,7,256]{2,1,0:T(8,128)} %param.12) | copy-start | bytes 64516
  3.3 16.9 %copy-start.2 = (f32[256]{0:T(256)S(1)}, f32[256]{0:T(256)}, u32[]{:S(2)}) copy-start(f32[256]{0:T(256)} %param.14) | copy-start | bytes 3076
  3.3 97.3 %all-to-all-start = ((bf16[32,200,128]{2,1,0:T(8,128)(2,1)}), bf16[32,200,128]{2,1,0:T(8,128)(2,1)S(1)}, u32[]{:S(2)}, u32[]{:S(2)}) async-start(bf16[32,200,128]{2,1,0:T(8,128)(2,1)} %pack.1), calls=%async_computation | async-start | bytes 3276800 | tf_op jit(solution)/shard_map/all_to_all | solution.py:309
  20.1 120.5 %copy-start.1 = (f32[256]{0:T(256)S(1)}, f32[256]{0:T(256)}, u32[]{:S(2)}) copy-start(f32[256]{0:T(256)} %param.15) | copy-start | bytes 3076
  133.9 13.2 %all-to-all-start.2 = ((f32[16,1,512]{2,1,0:T(1,128)}), f32[16,1,512]{2,1,0:T(1,128)S(1)}, u32[]{:S(2)}, u32[]{:S(2)}) async-start(f32[16,1,512]{2,1,0:T(1,128)} %power_rows.1), calls=%async_computation.2 | async-start | bytes 65536 | tf_op jit(solution)/shard_map/all_to_all | solution.py:309

commit v7 on v6

--- a/solution.py
+++ b/solution.py
@@ -24,8 +24,7 @@
 
 def pack_kernel(
     dest_hbm, count_ref, loaded_ref, lags_hbm, segments_hbm, out_ref,
-    rows_ref, turned_ref, notes_ref, dest_ref, lags_ref, segments_ref,
-    in_sems, out_sems, note_sems,
+    rows_ref, dest_ref, lags_ref, segments_ref, in_sems, note_sems,
 ):
     fetches = []
     small = [
@@ -42,7 +41,6 @@
         fetch.start()
         fetches.append(fetch)
 
-    sends = []
     for i in range(4):
         fetches[i].wait()
         pieces = [
@@ -50,12 +48,7 @@
             for t in range(3)
             for half in range(2)
         ]
-        turned_ref[i] = jnp.concatenate(pieces, axis=1).astype(bf16)
-        send = pltpu.make_async_copy(
-            turned_ref.at[i], out_ref.at[:, pl.ds(48 * i, 48), :], out_sems.at[i]
-        )
-        send.start()
-        sends.append(send)
+        out_ref[:, 48 * i : 48 * i + 48, :] = jnp.concatenate(pieces, axis=1).astype(bf16)
     for copy in small:
         copy.wait()
     lane = lax.broadcasted_iota(jnp.int32, (1, LANES), 1)
@@ -76,14 +69,8 @@
     for r in range(16):
         own = [lags[r : r + 1, LANES * j : LANES * j + LANES] for j in range(4)]
         note = jnp.concatenate(own + [common], axis=0).astype(bf16)
-        notes_ref[2 * r] = note
-        notes_ref[2 * r + 1] = note
-    send = pltpu.make_async_copy(notes_ref, out_ref.at[:, pl.ds(192, 8), :], out_sems.at[4])
-    send.start()
-    sends.append(send)
-
-    for send in sends:
-        send.wait()
+        out_ref[2 * r, 192:200, :] = note
+        out_ref[2 * r + 1, 192:200, :] = note
 
 
 def pack(dest, count, loaded, lags, segments):
@@ -95,17 +82,14 @@
     return pl.pallas_call(
         pack_kernel,
         in_specs=[far, scalars, far, far, far],
-        out_specs=far,
+        out_specs=pl.BlockSpec(memory_space=pltpu.VMEM),
         out_shape=jax.ShapeDtypeStruct((32, 200, LANES), bf16),
         scratch_shapes=[
             pltpu.VMEM((4, 3, 256, 256), bf16),
-            pltpu.VMEM((4, 32, 48, LANES), bf16),
-            pltpu.VMEM((32, 8, LANES), bf16),
             pltpu.SMEM((32,), jnp.int32),
             pltpu.VMEM((16, 512), bf16),
             pltpu.VMEM((4, LANES), jnp.int32),
             pltpu.SemaphoreType.DMA((4,)),
-            pltpu.SemaphoreType.DMA((5,)),
             pltpu.SemaphoreType.DMA((3,)),
         ],
         compiler_params=vmem(12),
@@ -114,10 +98,26 @@
 
 
 def conv_kernel(
-    table_ref, recv_ref, taps_ref, skip_ref, out_ref,
+    table_ref, recv_ref, filters_ref, skips_ref, out_ref,
     rows_ref, acc_ref, gate_ref, slots_ref, placed_ref, lags_ref, starts_ref, reach_ref,
+    sheet_ref, taps_ref,
 ):
     rows_ref[0:128, :] = jnp.zeros((128, 512), bf16)
+
+    sheet_ref[16:32, :] = jnp.zeros((16, 256), f32)
+    for t in range(3):
+        sheet_ref[TAPS * t : TAPS * t + TAPS, :] = filters_ref[t]
+    sheet_ref[3 * TAPS : 3 * TAPS + 1, :] = skips_ref[...]
+    first_channel = 8 * lax.axis_index("seq")
+    sheet = pltpu.roll(sheet_ref[...], (256 - first_channel) & 255, 1)[:, :LANES]
+    sheet = jnp.concatenate([sheet, jnp.zeros((96, LANES), f32)], axis=0)
+    sheet = jnp.transpose(sheet)[:8]
+    for t in range(3):
+        for j in range(TAPS):
+            value = sheet[:, TAPS * t + j : TAPS * t + j + 1]
+            taps_ref[j, 8 * t : 8 * t + 8, :] = jnp.broadcast_to(value, (8, LANES))
+    skip = jnp.broadcast_to(sheet[:, 3 * TAPS : 3 * TAPS + 1], (8, 256))
+    skip = jnp.concatenate([skip, skip], axis=0)
 
     def widen(s, carry):
         for pair in range(4):
@@ -127,7 +127,8 @@
                 slots_ref[8 * s + 2 * pair + 1, 8 * t : 8 * t + 8, :] = both[8:]
         return carry
 
-    lax.fori_loop(0, 32, widen, 0, unroll=2)
+    for s in range(32):
+        widen(s, 0)
     total = jnp.zeros((8, LANES), f32)
     for s in range(32):
         note = recv_ref[s, 192:200, :].astype(f32)
@@ -146,7 +147,9 @@
             begin = jnp.where(start <= here, start, begin)
         return begin
 
-    begin = lax.fori_loop(0, 8, latest, jnp.zeros((LANES, LANES), f32))
+    begin = jnp.zeros((LANES, LANES), f32)
+    for v in range(8):
+        begin = latest(v, begin)
     reach_ref[...] = jnp.minimum(here - begin, 6.0)
 
     lane = lax.broadcasted_iota(jnp.int32, (24, LANES), 1)
@@ -233,19 +236,18 @@
         else:
             acc_ref[begin:, :] += product
 
-    skip = jnp.broadcast_to(skip_ref[...], (16, 256))
-
     def finish(u, carry):
-        at = pl.ds(pl.multiple_of(16 * u, 16), 16)
-        here = pl.ds(pl.multiple_of(128 + 16 * u, 16), 16)
+        at = pl.ds(16 * u, 16)
+        here = pl.ds(128 + 16 * u, 16)
         total = acc_ref[at, :] + skip * rows_ref[here, 0:256].astype(f32)
         out_ref[u] = (gate_ref[u].astype(f32) * total).astype(bf16)
         return carry
 
-    lax.fori_loop(0, 32, finish, 0, unroll=4)
-
-
-def conv_rows(table, recv, taps, skip):
+    for u in range(32):
+        finish(u, 0)
+
+
+def conv_rows(table, recv, filters, skips):
     whole = pl.BlockSpec(memory_space=pltpu.VMEM)
     return pl.pallas_call(
         conv_kernel,
@@ -261,10 +263,12 @@
             pltpu.VMEM((32, 8, LANES), f32),
             pltpu.VMEM((LANES, LANES), f32),
             pltpu.VMEM((LANES, LANES), f32),
+            pltpu.VMEM((32, 256), f32),
+            pltpu.VMEM((TAPS, 24, LANES), f32),
         ],
         compiler_params=vmem(24),
         name="conv_rows",
-    )(table, recv, taps, skip)
+    )(table, recv, filters, skips)
 
 
 def power_kernel(in_ref, out_ref):
@@ -292,8 +296,8 @@
     gain = gain_ref[...]
     for half in range(2):
         block = in_ref[:, 8 * half : 8 * half + 8, :].astype(f32).reshape(256, 256)
-        block = block * scale[:, 256 * half : 256 * half + 256] * gain
-        out_ref[256 * half : 256 * half + 256, :] = jnp.transpose(block).astype(bf16)
+        block = jnp.transpose(block * scale[:, 256 * half : 256 * half + 256])
+        out_ref[256 * half : 256 * half + 256, :] = (block * gain).astype(bf16)
 
 
 def scale_rows(rows, power, gain):
@@ -312,7 +316,6 @@
 def local(
     loaded, dest_tiles, tile_counts, segments, short_filters, long_filters, skip_gain, norm_gain
 ):
-    position = lax.axis_index("seq")
     recv = exchange(
         pack(dest_tiles, tile_counts, loaded, long_filters, segments.reshape(4, LANES)), "seq"
     )
@@ -325,16 +328,10 @@
         jnp.where(placed[None, :] == tiles[:, None], slot_ids[None, :], 0), axis=1
     ).astype(jnp.int32)
 
-    taps = lax.dynamic_slice_in_dim(short_filters, position * 8, 8, 2)
-    taps = jnp.broadcast_to(taps[..., None], (3, TAPS, 8, LANES))
-    taps = jnp.transpose(taps, (1, 0, 2, 3)).reshape(TAPS, 24, LANES)
-    skip = lax.dynamic_slice_in_dim(skip_gain, position * 8, 8, 0)
-    skip = jnp.tile(skip, 2)[:, None]
-
-    gated = conv_rows(table, recv, taps, skip)
+    gated = conv_rows(table, recv, short_filters, skip_gain.reshape(1, 256))
     mine = exchange(gated, "seq")
     every = exchange(power_rows(mine), "chan")
-    return scale_rows(mine, every, norm_gain[:, None])
+    return scale_rows(mine, every, norm_gain.reshape(1, 256))
 
 
 def solution(mesh):

time: 148 us -> 147 us (level)
  blocking collectives: 25.4 us -> 136 us
  waiting for transfers between devices: 86.4 us -> 0 us
  starting transfers between devices: 23.5 us -> 0 us
  Pallas kernels: 11 us -> 9.29 us
    all_to_all x1 -> x3, blocking collectives: 25.4 us -> 136 us  [exchange(): return lax.all_to_all(block, axis, split_axis=0, concat_axis=0, tiled=True)]
    all_to_all x2 -> x0, waiting for transfers between devices: 86.4 us -> none  [exchange(): return lax.all_to_all(block, axis, split_axis=0, concat_axis=0, tiled=True)]
    all_to_all x2 -> x0, starting transfers between devices: 23.5 us -> none  [exchange(): return lax.all_to_all(block, axis, split_axis=0, concat_axis=0, tiled=True)]
  transfers between devices with their start and end apart: 2 -> 0, of which waited for: 2 -> 0; matrix products, arithmetic and copies ran while one was open for 0% -> 0% of each run, Pallas kernels for 0% -> 0%
where the time goes in v7:
time: 147 us
  blocking collectives  136 us (93%)
  Pallas kernels  9.29 us (6%)
    all_to_all x3, blocking collectives, exchange(): return lax.all_to_all(block, axis, split_axis=0, concat_axis=0, tiled=True)  136 us
    pallas_call x1, Pallas kernels, conv_rows(): pl.pallas_call(conv_kernel, in_specs=[pl.BlockSpec(memory_space=pltpu.SME...  6.38 us

profile of v7, /device:TPU:1, one launch (start us, length us, event | category | flops | bytes accessed | tf_op | source)
XLA Modules:
  0.0 146.5 jit_solution(18154552403890960107)
XLA Ops:
  0.7 1.9 %pack.1 = bf16[32,200,128]{2,1,0:T(8,128)(2,1)S(1)} custom-call(s32[32]{0:T(128)} %dest_hbm.1, s32[1]{0:T(128)S(6)} %copy.9.count_ref, bf16[3,1024,256]{2,1,0:T(8,128)(2,1)} %loaded_ref.1, bf16[16,512]{1,0:T(8,128)(2,1)} %lags_hbm.1, s32[4,128]{1,0:T(4,128)} %bitcast.7), custom_call_target="tpu_custom_call" | custom-call | tf_op jit(solution)/shard_map/pack/pallas_call | solution.py:82
  2.6 0.0 copy-start
  2.6 0.0 copy-start.1
  2.6 97.9 %all_to_all.15.recv_ref = bf16[32,200,128]{2,1,0:T(8,128)(2,1)S(1)} all-to-all(bf16[32,200,128]{2,1,0:T(8,128)(2,1)S(1)} %pack.1), channel_id=1, replica_groups=mesh['seq'=32,'chan'=16] {'seq'}, dimensions={0} | all-to-all | bytes 3276800 | tf_op jit(solution)/shard_map/all_to_all | solution.py:313
  100.5 0.0 copy-start.2
  100.5 0.1 slice_add_fusion
  100.6 0.1 eq.15
  100.7 0.3 select_reduce_fusion.table_ref
  101.0 0.0 copy-done
  101.0 0.0 copy-done.1
  101.0 6.4 %conv_rows.1 = bf16[32,16,256]{2,1,0:T(8,128)(2,1)S(1)} custom-call(s32[512]{0:T(512)S(1)} %select_reduce_fusion.table_ref, bf16[32,200,128]{2,1,0:T(8,128)(2,1)S(1)} %all_to_all.15.recv_ref, f32[3,7,256]{2,1,0:T(8,128)S(1)} %copy-done, f32[1,256]{1,0:T(1,128)S(1)} %bitcast.4), custom_call_target="tpu_custom_call" | custom-call | tf_op jit(solution)/shard_map/conv_rows/pallas_call | solution.py:252
  107.4 25.1 %all_to_all.16.in_ref = bf16[32,16,256]{2,1,0:T(8,128)(2,1)S(1)} all-to-all(bf16[32,16,256]{2,1,0:T(8,128)(2,1)S(1)} %conv_rows.1), channel_id=1, replica_groups=mesh['seq'=32,'chan'=16] {'seq'}, dimensions={0} | all-to-all | bytes 524288 | tf_op jit(solution)/shard_map/all_to_all | solution.py:313
  132.5 13.0 %all_to_all.17.power_ref = f32[16,1,512]{2,1,0:T(1,128)S(1)} all-to-all(f32[16,1,512]{2,1,0:T(1,128)S(1)} %power_rows.1), channel_id=1, replica_groups=mesh['seq'=32,'chan'=16] {'chan'}, dimensions={0} | all-to-all | bytes 65536 | tf_op jit(solution)/shard_map/all_to_all | solution.py:313
  145.6 0.0 copy-done.2
  145.6 0.9 scale_rows.1
  (2 shorter events, 0.1 us)
Async XLA Ops:
  2.6 98.4 %copy-start = (f32[3,7,256]{2,1,0:T(8,128)S(1)}, f32[3,7,256]{2,1,0:T(8,128)}, u32[]{:S(2)}) copy-start(f32[3,7,256]{2,1,0:T(8,128)} %filters_ref.1) | copy-start | bytes 64516
  2.6 98.4 %copy-start.1 = (f32[256]{0:T(256)S(1)}, f32[256]{0:T(256)}, u32[]{:S(2)}) copy-start(f32[256]{0:T(256)} %param.14) | copy-start | bytes 3076
  100.5 45.1 %copy-start.2 = (f32[256]{0:T(256)S(1)}, f32[256]{0:T(256)}, u32[]{:S(2)}) copy-start(f32[256]{0:T(256)} %param.15) | copy-start | bytes 3076

commit v8 on v7

--- a/solution.py
+++ b/solution.py
@@ -52,11 +52,11 @@
     for copy in small:
         copy.wait()
     lane = lax.broadcasted_iota(jnp.int32, (1, LANES), 1)
-    line = jnp.zeros((1, LANES), jnp.int32)
+    high = jnp.full((1, LANES), 16 * 63, jnp.int32)
+    low = jnp.zeros((1, LANES), jnp.int32)
     for j in range(32):
-        high = jnp.where(j < count_ref[0], dest_ref[j] >> 4, 63)
-        line = jnp.where(lane == j, high, line)
-        line = jnp.where(lane == 32 + j, dest_ref[j] & 15, line)
+        high = jnp.where((lane == j) & (j < count_ref[0]), dest_ref[j] & 496, high)
+        low = jnp.where(lane == j, dest_ref[j] & 15, low)
     index = lax.broadcasted_iota(jnp.int32, (LANES, LANES), 0)
     fewer = jnp.zeros((LANES, LANES), f32)
     for j in range(4):
@@ -64,7 +64,9 @@
     below = jnp.sum(fewer, axis=1, keepdims=True).astype(jnp.int32)
     below = jnp.where(index[:, :1] < 64, below >> 4, below & 15).astype(f32)
     below = jnp.transpose(jnp.broadcast_to(below, (LANES, LANES)))[:1]
-    common = jnp.concatenate([below, line.astype(f32), jnp.zeros((2, LANES), f32)], axis=0)
+    common = jnp.concatenate(
+        [below, high.astype(f32), low.astype(f32), jnp.zeros((1, LANES), f32)], axis=0
+    )
     lags = lags_ref[...].astype(f32)
     for r in range(16):
         own = [lags[r : r + 1, LANES * j : LANES * j + LANES] for j in range(4)]
@@ -320,8 +322,8 @@
         pack(dest_tiles, tile_counts, loaded, long_filters, segments.reshape(4, LANES)), "seq"
     )
 
-    slots = recv[:, 197].astype(jnp.int32)
-    placed = (slots[:, 0:32] * 16 + slots[:, 32:64]).reshape(-1)
+    placed = (recv[:, 197, :32].astype(f32) + recv[:, 198, :32].astype(f32)).astype(jnp.int32)
+    placed = placed.reshape(-1)
     tiles = jnp.arange(512, dtype=jnp.int32)
     slot_ids = jnp.arange(1024, dtype=jnp.int32)
     table = jnp.sum(

time: 147 us -> 147 us (level)
  no operation moved by 1% of the time
where the time goes in v8:
time: 147 us; the launch traced here: 146 us
  blocking collectives  136 us (93%)
  Pallas kernels  9.28 us (6%)
    all_to_all x3, blocking collectives, exchange(): return lax.all_to_all(block, axis, split_axis=0, concat_axis=0, tiled=True)  136 us
    pallas_call x1, Pallas kernels, conv_rows(): pl.pallas_call(conv_kernel, in_specs=[pl.BlockSpec(memory_space=pltpu.SME...  6.38 us

profile of v8, /device:TPU:1, one launch (start us, length us, event | category | flops | bytes accessed | tf_op | source)
XLA Modules:
  0.0 146.5 jit_solution(16721889629780883622)
XLA Ops:
  0.7 1.9 %pack.1 = bf16[32,200,128]{2,1,0:T(8,128)(2,1)S(1)} custom-call(s32[32]{0:T(128)} %dest_hbm.1, s32[1]{0:T(128)S(6)} %copy.9.count_ref, bf16[3,1024,256]{2,1,0:T(8,128)(2,1)} %loaded_ref.1, bf16[16,512]{1,0:T(8,128)(2,1)} %lags_hbm.1, s32[4,128]{1,0:T(4,128)} %bitcast.5), custom_call_target="tpu_custom_call" | custom-call | tf_op jit(solution)/shard_map/pack/pallas_call | solution.py:84
  2.6 0.0 copy-start
  2.6 0.0 copy-start.1
  2.6 97.9 %all_to_all.15.recv_ref = bf16[32,200,128]{2,1,0:T(8,128)(2,1)S(1)} all-to-all(bf16[32,200,128]{2,1,0:T(8,128)(2,1)S(1)} %pack.1), channel_id=1, replica_groups=mesh['seq'=32,'chan'=16] {'seq'}, dimensions={0} | all-to-all | bytes 3276800 | tf_op jit(solution)/shard_map/all_to_all | solution.py:315
  100.5 0.0 copy-start.2
  100.5 0.1 fusion.2
  100.6 0.1 convert_element_type.29
  100.6 0.3 select_reduce_fusion.table_ref
  100.9 0.0 copy-done
  100.9 0.0 copy-done.1
  100.9 6.4 %conv_rows.1 = bf16[32,16,256]{2,1,0:T(8,128)(2,1)S(1)} custom-call(s32[512]{0:T(512)S(1)} %select_reduce_fusion.table_ref, bf16[32,200,128]{2,1,0:T(8,128)(2,1)S(1)} %all_to_all.15.recv_ref, f32[3,7,256]{2,1,0:T(8,128)S(1)} %copy-done, f32[1,256]{1,0:T(1,128)S(1)} %bitcast.3), custom_call_target="tpu_custom_call" | custom-call | tf_op jit(solution)/shard_map/conv_rows/pallas_call | solution.py:254
  107.3 25.1 %all_to_all.16.in_ref = bf16[32,16,256]{2,1,0:T(8,128)(2,1)S(1)} all-to-all(bf16[32,16,256]{2,1,0:T(8,128)(2,1)S(1)} %conv_rows.1), channel_id=1, replica_groups=mesh['seq'=32,'chan'=16] {'seq'}, dimensions={0} | all-to-all | bytes 524288 | tf_op jit(solution)/shard_map/all_to_all | solution.py:315
  132.5 13.0 %all_to_all.17.power_ref = f32[16,1,512]{2,1,0:T(1,128)S(1)} all-to-all(f32[16,1,512]{2,1,0:T(1,128)S(1)} %power_rows.1), channel_id=1, replica_groups=mesh['seq'=32,'chan'=16] {'chan'}, dimensions={0} | all-to-all | bytes 65536 | tf_op jit(solution)/shard_map/all_to_all | solution.py:315
  145.5 0.0 copy-done.2
  145.5 0.9 scale_rows.1
  (1 shorter events, 0.0 us)
Async XLA Ops:
  2.6 98.3 %copy-start = (f32[3,7,256]{2,1,0:T(8,128)S(1)}, f32[3,7,256]{2,1,0:T(8,128)}, u32[]{:S(2)}) copy-start(f32[3,7,256]{2,1,0:T(8,128)} %filters_ref.1) | copy-start | bytes 64516
  2.6 98.3 %copy-start.1 = (f32[256]{0:T(256)S(1)}, f32[256]{0:T(256)}, u32[]{:S(2)}) copy-start(f32[256]{0:T(256)} %param.14) | copy-start | bytes 3076
  100.5 45.1 %copy-start.2 = (f32[256]{0:T(256)S(1)}, f32[256]{0:T(256)}, u32[]{:S(2)}) copy-start(f32[256]{0:T(256)} %param.15) | copy-start | bytes 3076

commit v9 on v8

--- a/solution.py
+++ b/solution.py
@@ -170,16 +170,16 @@
     shift = (ahead == LANES + (lag & 127) - (lag >> 7) - 1).astype(bf16)
 
     def short(u, last):
-        now = placed_ref[pl.ds(8 * u + 1, 8)]
+        now = placed_ref[pl.ds(16 * u + 1, 16)]
         both = jnp.concatenate(
-            [placed_ref[pl.ds(8 * u, 8)].reshape(192, LANES), now.reshape(192, LANES)], axis=1
+            [placed_ref[pl.ds(16 * u, 16)].reshape(384, LANES), now.reshape(384, LANES)], axis=1
         )
         delayed = jnp.dot(both, shift, preferred_element_type=f32)
-        for v in range(8 // 4):
+        for v in range(16 // 4):
             mixed = []
             gates = []
             for k in range(4 * v, 4 * v + 4):
-                limit = jnp.broadcast_to(reach_ref[pl.ds(8 * u + k, 1), :], (24, LANES))
+                limit = jnp.broadcast_to(reach_ref[pl.ds(16 * u + k, 1), :], (24, LANES))
                 total = now[k].astype(f32) * taps_ref[0]
                 for j in range(1, TAPS):
                     part = delayed[24 * k : 24 * k + 24, LANES * (j - 1) : LANES * j]
@@ -188,10 +188,10 @@
                 mixed.append(total[8:16] * total[16:])
             first = jnp.concatenate(mixed[:2], axis=1)
             second = jnp.concatenate(mixed[2:], axis=1)
-            at = pl.ds(128 + 32 * u + 16 * v, 16)
+            at = pl.ds(128 + 64 * u + 16 * v, 16)
             rows_ref[at, 0:256] = jnp.concatenate([first, second], axis=0).astype(bf16)
             rows_ref[at, 256:512] = jnp.concatenate([last, first], axis=0).astype(bf16)
-            gate_ref[2 * u + v] = jnp.concatenate(
+            gate_ref[4 * u + v] = jnp.concatenate(
                 [jnp.concatenate(gates[:2], axis=1), jnp.concatenate(gates[2:], axis=1)], axis=0
             ).astype(bf16)
             last = second
@@ -199,9 +199,9 @@
 
     placed_ref[0] = jnp.zeros((24, LANES), bf16)
     last = jnp.zeros((8, 256), f32)
-    for u in range(16):
-        for k in range(8):
-            gather(8 * u + k)
+    for u in range(8):
+        for k in range(16):
+            gather(16 * u + k)
         last = short(u, last)
 
     upper = col >= row

time: 147 us -> 148 us (level)
  no operation moved by 1% of the time
where the time goes in v9:
time: 148 us; the launch traced here: 147 us
  blocking collectives  136 us (92%)
  Pallas kernels  10 us (7%)
    all_to_all x3, blocking collectives, exchange(): return lax.all_to_all(block, axis, split_axis=0, concat_axis=0, tiled=True)  136 us
    pallas_call x1, Pallas kernels, conv_rows(): pl.pallas_call(conv_kernel, in_specs=[pl.BlockSpec(memory_space=pltpu.SME...  7.11 us

profile of v9, /device:TPU:1, one launch (start us, length us, event | category | flops | bytes accessed | tf_op | source)
XLA Modules:
  0.0 147.2 jit_solution(11859723712233817547)
XLA Ops:
  0.7 1.9 %pack.1 = bf16[32,200,128]{2,1,0:T(8,128)(2,1)S(1)} custom-call(s32[32]{0:T(128)} %dest_hbm.1, s32[1]{0:T(128)S(6)} %copy.9.count_ref, bf16[3,1024,256]{2,1,0:T(8,128)(2,1)} %loaded_ref.1, bf16[16,512]{1,0:T(8,128)(2,1)} %lags_hbm.1, s32[4,128]{1,0:T(4,128)} %bitcast.5), custom_call_target="tpu_custom_call" | custom-call | tf_op jit(solution)/shard_map/pack/pallas_call | solution.py:84
  2.6 0.0 copy-start
  2.6 0.0 copy-start.1
  2.6 97.9 %all_to_all.15.recv_ref = bf16[32,200,128]{2,1,0:T(8,128)(2,1)S(1)} all-to-all(bf16[32,200,128]{2,1,0:T(8,128)(2,1)S(1)} %pack.1), channel_id=1, replica_groups=mesh['seq'=32,'chan'=16] {'seq'}, dimensions={0} | all-to-all | bytes 3276800 | tf_op jit(solution)/shard_map/all_to_all | solution.py:315
  100.5 0.0 copy-start.2
  100.5 0.1 fusion.2
  100.6 0.1 convert_element_type.29
  100.6 0.3 select_reduce_fusion.table_ref
  100.9 0.0 copy-done
  100.9 0.0 copy-done.1
  100.9 7.1 %conv_rows.1 = bf16[32,16,256]{2,1,0:T(8,128)(2,1)S(1)} custom-call(s32[512]{0:T(512)S(1)} %select_reduce_fusion.table_ref, bf16[32,200,128]{2,1,0:T(8,128)(2,1)S(1)} %all_to_all.15.recv_ref, f32[3,7,256]{2,1,0:T(8,128)S(1)} %copy-done, f32[1,256]{1,0:T(1,128)S(1)} %bitcast.3), custom_call_target="tpu_custom_call" | custom-call | tf_op jit(solution)/shard_map/conv_rows/pallas_call | solution.py:254
  108.1 25.1 %all_to_all.16.in_ref = bf16[32,16,256]{2,1,0:T(8,128)(2,1)S(1)} all-to-all(bf16[32,16,256]{2,1,0:T(8,128)(2,1)S(1)} %conv_rows.1), channel_id=1, replica_groups=mesh['seq'=32,'chan'=16] {'seq'}, dimensions={0} | all-to-all | bytes 524288 | tf_op jit(solution)/shard_map/all_to_all | solution.py:315
  133.2 13.0 %all_to_all.17.power_ref = f32[16,1,512]{2,1,0:T(1,128)S(1)} all-to-all(f32[16,1,512]{2,1,0:T(1,128)S(1)} %power_rows.1), channel_id=1, replica_groups=mesh['seq'=32,'chan'=16] {'chan'}, dimensions={0} | all-to-all | bytes 65536 | tf_op jit(solution)/shard_map/all_to_all | solution.py:315
  146.3 0.0 copy-done.2
  146.3 0.9 scale_rows.1
  (1 shorter events, 0.0 us)
Async XLA Ops:
  2.6 98.3 %copy-start = (f32[3,7,256]{2,1,0:T(8,128)S(1)}, f32[3,7,256]{2,1,0:T(8,128)}, u32[]{:S(2)}) copy-start(f32[3,7,256]{2,1,0:T(8,128)} %filters_ref.1) | copy-start | bytes 64516
  2.6 98.3 %copy-start.1 = (f32[256]{0:T(256)S(1)}, f32[256]{0:T(256)}, u32[]{:S(2)}) copy-start(f32[256]{0:T(256)} %param.14) | copy-start | bytes 3076
  100.5 45.8 %copy-start.2 = (f32[256]{0:T(256)S(1)}, f32[256]{0:T(256)}, u32[]{:S(2)}) copy-start(f32[256]{0:T(256)} %param.15) | copy-start | bytes 3076

commit v10 on v8

--- a/solution.py
+++ b/solution.py
@@ -292,20 +292,32 @@
     )(rows)
 
 
-def scale_kernel(in_ref, power_ref, gain_ref, out_ref):
+def scale_kernel(in_ref, power_ref, gain_ref, out_ref, turned_ref, sems):
     power = jnp.sum(power_ref[...], axis=0)
     scale = lax.rsqrt(power / 4096.0 + 1e-06)
     gain = gain_ref[...]
+    sends = []
     for half in range(2):
         block = in_ref[:, 8 * half : 8 * half + 8, :].astype(f32).reshape(256, 256)
         block = jnp.transpose(block * scale[:, 256 * half : 256 * half + 256])
-        out_ref[256 * half : 256 * half + 256, :] = (block * gain).astype(bf16)
+        turned_ref[half] = (block * gain).astype(bf16)
+        send = pltpu.make_async_copy(
+            turned_ref.at[half], out_ref.at[pl.ds(256 * half, 256), :], sems.at[half]
+        )
+        send.start()
+        sends.append(send)
+    for send in sends:
+        send.wait()
 
 
 def scale_rows(rows, power, gain):
+    whole = pl.BlockSpec(memory_space=pltpu.VMEM)
     return pl.pallas_call(
         scale_kernel,
+        in_specs=[whole] * 3,
+        out_specs=pl.BlockSpec(memory_space=pltpu.HBM),
         out_shape=jax.ShapeDtypeStruct((512, 256), bf16),
+        scratch_shapes=[pltpu.VMEM((2, 256, 256), bf16), pltpu.SemaphoreType.DMA((2,))],
         compiler_params=vmem(4),
         name="scale_rows",
     )(rows, power, gain)

time: 147 us -> 147 us (level)
  no operation moved by 1% of the time
where the time goes in v10:
time: 147 us; the launch traced here: 146 us
  blocking collectives  136 us (93%)
  Pallas kernels  9.25 us (6%)
    all_to_all x3, blocking collectives, exchange(): return lax.all_to_all(block, axis, split_axis=0, concat_axis=0, tiled=True)  136 us
    pallas_call x1, Pallas kernels, conv_rows(): pl.pallas_call(conv_kernel, in_specs=[pl.BlockSpec(memory_space=pltpu.SME...  6.37 us

profile of v10, /device:TPU:1, one launch (start us, length us, event | category | flops | bytes accessed | tf_op | source)
XLA Modules:
  0.0 146.4 jit_solution(6643890606583524872)
XLA Ops:
  0.7 1.9 %pack.1 = bf16[32,200,128]{2,1,0:T(8,128)(2,1)S(1)} custom-call(s32[32]{0:T(128)} %dest_hbm.1, s32[1]{0:T(128)S(6)} %copy.9.count_ref, bf16[3,1024,256]{2,1,0:T(8,128)(2,1)} %loaded_ref.1, bf16[16,512]{1,0:T(8,128)(2,1)} %lags_hbm.1, s32[4,128]{1,0:T(4,128)} %bitcast.5), custom_call_target="tpu_custom_call" | custom-call | tf_op jit(solution)/shard_map/pack/pallas_call | solution.py:84
  2.6 0.0 copy-start
  2.6 0.0 copy-start.1
  2.6 97.9 %all_to_all.15.recv_ref = bf16[32,200,128]{2,1,0:T(8,128)(2,1)S(1)} all-to-all(bf16[32,200,128]{2,1,0:T(8,128)(2,1)S(1)} %pack.1), channel_id=1, replica_groups=mesh['seq'=32,'chan'=16] {'seq'}, dimensions={0} | all-to-all | bytes 3276800 | tf_op jit(solution)/shard_map/all_to_all | solution.py:327
  100.5 0.0 copy-start.2
  100.5 0.1 fusion.2
  100.6 0.1 convert_element_type.29
  100.6 0.3 select_reduce_fusion.table_ref
  100.9 0.0 copy-done
  100.9 0.0 copy-done.1
  100.9 6.4 %conv_rows.1 = bf16[32,16,256]{2,1,0:T(8,128)(2,1)S(1)} custom-call(s32[512]{0:T(512)S(1)} %select_reduce_fusion.table_ref, bf16[32,200,128]{2,1,0:T(8,128)(2,1)S(1)} %all_to_all.15.recv_ref, f32[3,7,256]{2,1,0:T(8,128)S(1)} %copy-done, f32[1,256]{1,0:T(1,128)S(1)} %bitcast.3), custom_call_target="tpu_custom_call" | custom-call | tf_op jit(solution)/shard_map/conv_rows/pallas_call | solution.py:254
  107.3 25.1 %all_to_all.16.in_ref = bf16[32,16,256]{2,1,0:T(8,128)(2,1)S(1)} all-to-all(bf16[32,16,256]{2,1,0:T(8,128)(2,1)S(1)} %conv_rows.1), channel_id=1, replica_groups=mesh['seq'=32,'chan'=16] {'seq'}, dimensions={0} | all-to-all | bytes 524288 | tf_op jit(solution)/shard_map/all_to_all | solution.py:327
  132.5 13.0 %all_to_all.17.power_ref = f32[16,1,512]{2,1,0:T(1,128)S(1)} all-to-all(f32[16,1,512]{2,1,0:T(1,128)S(1)} %power_rows.1), channel_id=1, replica_groups=mesh['seq'=32,'chan'=16] {'chan'}, dimensions={0} | all-to-all | bytes 65536 | tf_op jit(solution)/shard_map/all_to_all | solution.py:327
  145.5 0.0 copy-done.2
  145.5 0.9 scale_rows.1
  (1 shorter events, 0.0 us)
Async XLA Ops:
  2.6 98.3 %copy-start = (f32[3,7,256]{2,1,0:T(8,128)S(1)}, f32[3,7,256]{2,1,0:T(8,128)}, u32[]{:S(2)}) copy-start(f32[3,7,256]{2,1,0:T(8,128)} %filters_ref.1) | copy-start | bytes 64516
  2.6 98.3 %copy-start.1 = (f32[256]{0:T(256)S(1)}, f32[256]{0:T(256)}, u32[]{:S(2)}) copy-start(f32[256]{0:T(256)} %param.14) | copy-start | bytes 3076
  100.5 45.1 %copy-start.2 = (f32[256]{0:T(256)S(1)}, f32[256]{0:T(256)}, u32[]{:S(2)}) copy-start(f32[256]{0:T(256)} %param.15) | copy-start | bytes 3076
